TPU v7x, 128 devices: a whole 4x4x4 slice. The times are simulated.
128 devices in a mesh: ord: 64 (over x, y, z), rhs: 2 (over core).
Axes of the slice: x: 4, y: 4, z: 4, core: 2. Of those that a mesh axis runs over, the one named last changes fastest.
Arguments:
- rhs_blocks: float32 [512, 640, 128], P('ord', None, 'rhs'), may hold values from -6 to 6
- rhs_border: float32 [512, 128], P(None, 'rhs'), may hold values from -6 to 6
- start_blocks: float32 [512, 640, 128], P('ord', None, 'rhs'), may hold values from -3 to 3
- start_border: float32 [512, 128], P(None, 'rhs'), may hold values from -3 to 3
- diag_blocks: bfloat16 [512, 640, 640], P('ord'), may hold values from -1 to 9
- block_inverses: bfloat16 [512, 640, 640], P('ord'), may hold values from -6 to 6
- couplings: bfloat16 [512, 640, 640], P('ord'), may hold values from -0.125 to 0.125
- border_couplings: bfloat16 [512, 640, 512], P('ord'), may hold values from -0.009765625 to 0.009765625
- border_block: bfloat16 [512, 512], replicated, may hold values from -1 to 9
- schur_inverse: float32 [512, 512], replicated, may hold values from -6 to 6
- row_counts: int32 [512], P('ord'), may hold values from 1 to 640, as said below
Outputs:
- solution_blocks: float32 [512, 640, 128], P('ord', None, 'rhs')
- solution_border: float32 [512, 128], P(None, 'rhs')
Inputs may be any that keep to these rules, and one draw needn't show every extreme that they name: row_counts[m] is the number of live rows of order block m; block 0 has exactly 640 rows and the counts fall with the order to about a third of 640.
All inputs are finite; a program needn't handle non-finite values.
Results may differ from a plain program's by a relative error of at most 0.0035.
Values may be sent and summed in bfloat16 or wider, within the bound.
No kernel may reach another device: no remote copies, remote signals or barrier semaphores. Data moves between devices by JAX's collectives and lax.ppermute only.
A program may use at most 128 MiB of HBM per device.

v0:
```python
import functools

import jax
import jax.numpy as jnp
from jax import lax
from jax.sharding import Mesh
from jax.sharding import PartitionSpec as P

ITERS = 3
ORD = ("ord_0", "ord_1", "ord_2")
ORD_RHS = ("ord_0", "ord_1", "ord_2", "rhs")


def shifted(value, axis, steps):
    count = lax.axis_size(axis)
    leading, last = (max(0, -steps), min(count, count - steps))
    return lax.ppermute(value, axis, [(source, source + steps) for source in range(leading, last)])


def total_of_pieces(array, axis):
    parts = lax.all_gather(array, axis)
    return parts.sum(axis=0)


def cut_along(array, dim, count):
    before, after = (array.shape[:dim], array.shape[dim + 1 :])
    return jnp.moveaxis(array.reshape(*before, count, -1, *after), dim, 0)


def summed_on_arrival(array, axis, dim):
    count = lax.axis_size(axis)
    parts = lax.all_to_all(cut_along(array, dim, count), axis, 0, 0, tiled=True)
    return jnp.sum(parts, axis=0)


def laid_out(parts, dim):
    lengths = list(parts.shape[1:])
    lengths[dim] *= parts.shape[0]
    return jnp.moveaxis(parts, 0, dim).reshape(lengths)


def from_everyone(array, axis):
    count = lax.axis_size(axis)
    return lax.all_to_all(
        jnp.broadcast_to(array[None], (count, *array.shape)), axis, 0, 0, tiled=True
    )


def gathered_copies(array, axis, dim):
    return laid_out(from_everyone(array, axis), dim)


def over_axes(array, axes):
    return functools.reduce(lax.psum, axes, array)


def batched(matrices, vectors):
    return jnp.einsum("sij,sjc->sic", matrices, vectors, preferred_element_type=jnp.float32)


def shards(
    rhs_blocks,
    rhs_border,
    start_blocks,
    start_border,
    diag_blocks,
    block_inverses,
    couplings,
    border_couplings,
    border_block,
    schur_inverse,
    row_counts,
):
    slot_count = rhs_blocks.shape[0]
    row_total = rhs_blocks.shape[1]
    live_rows = (
        lax.broadcasted_iota(jnp.int32, (slot_count, row_total), 1) < row_counts[:, None]
    ).astype(jnp.float32)[:, :, None]

    def operate(state, state_border, against):
        narrow = state.astype(jnp.bfloat16)
        narrow_border = state_border.astype(jnp.bfloat16)
        upper = shifted(narrow[:1], ORD, -1)
        ahead = batched(couplings, jnp.concatenate([narrow[1:], upper], 0))
        transposed = jnp.einsum(
            "sji,sjc->sic", couplings, narrow, preferred_element_type=jnp.float32
        )
        lower = shifted(transposed[slot_count - 1 :].astype(jnp.bfloat16), ORD, 1).astype(
            jnp.float32
        )
        behind = jnp.concatenate([lower, transposed[:-1]], 0)
        from_border = jnp.einsum(
            "sib,bc->sic", border_couplings, narrow_border, preferred_element_type=jnp.float32
        )
        applied = live_rows * (batched(diag_blocks, narrow) + ahead + behind + from_border)
        gathered = jnp.einsum(
            "sib,sic->bc", border_couplings, narrow, preferred_element_type=jnp.float32
        )
        block_numerator = jnp.sum(against * applied)
        block_denominator = jnp.sum(applied * applied)
        gathered = total_of_pieces(gathered, ORD)
        applied_border = (
            jnp.dot(border_block, narrow_border, preferred_element_type=jnp.float32) + gathered
        )
        return (applied, applied_border, block_numerator, block_denominator)

    solution = live_rows * start_blocks
    solution_border = start_border
    applied, applied_border, unused_num, unused_den = operate(
        solution, solution_border, jnp.zeros_like(solution)
    )
    residual = live_rows * rhs_blocks - applied
    resid_border = rhs_border - applied_border
    for iteration in range(ITERS):
        blockwise = live_rows * batched(block_inverses, residual.astype(jnp.bfloat16))
        border_sum = jnp.einsum(
            "sib,sic->bc",
            border_couplings,
            blockwise.astype(jnp.bfloat16),
            preferred_element_type=jnp.float32,
        )
        piece = summed_on_arrival(border_sum, ORD, 1)
        column_start = lax.axis_index(ORD) * piece.shape[1]
        target = lax.dynamic_slice_in_dim(resid_border, column_start, piece.shape[1], 1) - piece
        update_piece = jnp.dot(schur_inverse, target, precision=lax.Precision.HIGHEST)
        update_border = gathered_copies(update_piece, ORD, 1)
        lifted = jnp.einsum(
            "sib,bc->sic",
            border_couplings,
            update_border.astype(jnp.bfloat16),
            preferred_element_type=jnp.float32,
        ).astype(jnp.bfloat16)
        update = blockwise - live_rows * batched(block_inverses, lifted)
        update, update_border = (update, update_border)
        applied, applied_border, block_numerator, block_denominator = operate(
            update, update_border, residual
        )
        border_numerator = jnp.sum(resid_border * applied_border)
        border_denominator = jnp.sum(applied_border * applied_border)
        first_copy = (lax.axis_index(ORD) == 0).astype(jnp.float32)
        numerator, denominator = (
            over_axes(block_numerator + first_copy * border_numerator, ORD_RHS),
            over_axes(block_denominator + first_copy * border_denominator, ORD_RHS),
        )
        step_size = numerator / (denominator + 1e-06)
        solution = solution + step_size * update
        solution_border = solution_border + step_size * update_border
        residual = residual - step_size * applied
        resid_border = resid_border - step_size * applied_border
    return (solution, solution_border)


def solution(mesh):
    finer = Mesh(
        mesh.devices.reshape(4, 4, 4, mesh.shape["rhs"]), ("ord_0", "ord_1", "ord_2", "rhs")
    )
    return jax.shard_map(
        shards,
        mesh=finer,
        in_specs=(
            P(ORD, None, "rhs"),
            P(None, "rhs"),
            P(ORD, None, "rhs"),
            P(None, "rhs"),
            P(ORD, None, None),
            P(ORD, None, None),
            P(ORD, None, None),
            P(ORD, None, None),
            P(),
            P(),
            P(ORD),
        ),
        out_specs=(P(ORD, None, "rhs"), P(None, "rhs")),
        check_vma=False,
    )
```

profile of v0, /device:TPU:0, one launch (start us, length us, event | category | flops | bytes accessed | tf_op | source)
XLA Modules:
  0.0 635.6 jit_solution(12656153422983094226)
XLA Ops:
  23.4 5.2 fusion.86
  38.0 12.3 %all-to-all-start = ((f32[64,512,1]{1,2,0:T(1,128)}), f32[64,512,1]{1,2,0:T(1,128)S(1)}, u32[]{:S(2)}, u32[]{:S(2)}) async-start(f32[64,512,1]{1,2,0:T(1,128)} %copy.13), calls=%async_computation | async-start | bytes 262144 | tf_op jit(solution)/shard_map/all_to_all | solution.py:32
  50.5 10.1 %all-to-all-done = f32[64,512,1]{1,2,0:T(1,128)S(1)} async-done(((f32[64,512,1]{1,2,0:T(1,128)}), f32[64,512,1]{1,2,0:T(1,128)S(1)}, u32[]{:S(2)}, u32[]{:S(2)}) %all-to-all-start) | async-done | bytes 131104 | tf_op jit(solution)/shard_map/all_to_all | solution.py:32
  60.8 36.9 %all-gather.9.cloned.1.call-done = f32[32768,64]{0,1:T(8,128)} async-done(((f32[512,64]{0,1:T(8,128)}), f32[32768,64]{0,1:T(8,128)}) %all-gather.9.cloned.1.call-update) | async-done | bytes 8388624 | tf_op jit(solution)/shard_map/all_gather | solution.py:21
  97.7 8.3 %copy.22 = f32[8,8,64,512]{3,2,1,0:T(8,128)S(1)} copy(f32[8,8,64,512]{3,1,2,0:T(8,128)} %bitcast.289) | data formatting | bytes 16777216
  109.9 18.2 %all_to_all.30 = f32[64,512,1]{1,2,0:T(1,128)S(1)} all-to-all(f32[64,512,1]{1,2,0:T(1,128)S(1)} %broadcast_in_dim.6), channel_id=1, replica_groups=mesh['ord_0'=4,'ord_1'=4,'ord_2'=4,'rhs'=2] {'ord_0','ord_1','ord_2'}, dimensions={0} | all-to-all | bytes 262144 | tf_op jit(solution)/shard_map/all_to_all | solution.py:44
  154.3 59.8 %all-gather.11.cloned.1.call-done = f32[32768,64]{0,1:T(8,128)} async-done(((f32[512,64]{0,1:T(8,128)}), f32[32768,64]{0,1:T(8,128)}) %all-gather.11.cloned.1.call-update) | async-done | bytes 8388624 | tf_op jit(solution)/shard_map/all_gather | solution.py:21
  214.0 8.1 %copy.23 = f32[8,8,64,512]{3,2,1,0:T(8,128)S(1)} copy(f32[8,8,64,512]{3,1,2,0:T(8,128)} %bitcast.290) | data formatting | bytes 16777216
  228.7 11.0 %all-reduce.8 = (f32[]{:T(128)}, f32[]{:T(128)}) all-reduce(f32[]{:T(128)S(6)} %add.187, f32[]{:T(128)S(6)} %add.188), channel_id=1, replica_groups=mesh['ord_0'=4,'ord_1'=4,'ord_2'=4,'rhs'=2] {'ord_0'}, use_global_device_ids=true, to_apply=%region_5.0 | all-reduce | flops 2 | bytes 16 | tf_op jit(solution)/shard_map/psum | solution.py:54
  239.6 11.1 %all-reduce.5 = (f32[]{:T(128)}, f32[]{:T(128)}) all-reduce(f32[]{:T(128)} %get-tuple-element.30, f32[]{:T(128)} %get-tuple-element.31), channel_id=1, replica_groups=mesh['ord_0'=4,'ord_1'=4,'ord_2'=4,'rhs'=2] {'ord_1'}, use_global_device_ids=true, to_apply=%region_6.0 | all-reduce | flops 2 | bytes 16 | tf_op jit(solution)/shard_map/psum | solution.py:54
  250.8 9.1 %all-reduce.2 = (f32[]{:T(128)}, f32[]{:T(128)}) all-reduce(f32[]{:T(128)} %get-tuple-element.24, f32[]{:T(128)} %get-tuple-element.25), channel_id=1, replica_groups=mesh['ord_0'=4,'ord_1'=4,'ord_2'=4,'rhs'=2] {'ord_2'}, use_global_device_ids=true, to_apply=%region_7.0 | all-reduce | flops 2 | bytes 16 | tf_op jit(solution)/shard_map/psum | solution.py:54
  266.0 5.6 convolution_multiply_fusion.3
  273.5 5.6 all-to-all-start.2
  280.8 8.0 %all-to-all-done.2 = f32[64,512,1]{1,2,0:T(1,128)} async-done(((f32[64,512,1]{1,2,0:T(1,128)}), f32[64,512,1]{1,2,0:T(1,128)}, u32[]{:S(2)}, u32[]{:S(2)}) %all-to-all-start.2) | async-done | bytes 131104 | tf_op jit(solution)/shard_map/all_to_all | solution.py:32
  291.8 14.6 %all_to_all.31 = f32[64,512,1]{1,2,0:T(1,128)S(1)} all-to-all(f32[64,512,1]{1,2,0:T(1,128)S(1)} %broadcast_in_dim.7), channel_id=1, replica_groups=mesh['ord_0'=4,'ord_1'=4,'ord_2'=4,'rhs'=2] {'ord_0','ord_1','ord_2'}, dimensions={0} | all-to-all | bytes 262144 | tf_op jit(solution)/shard_map/all_to_all | solution.py:44
  317.3 4.4 convolution_bitcast_fusion.2
  335.1 59.8 %all-gather.13.cloned.1.call-done = f32[32768,64]{0,1:T(8,128)} async-done(((f32[512,64]{0,1:T(8,128)}), f32[32768,64]{0,1:T(8,128)}) %all-gather.13.cloned.1.call-update) | async-done | bytes 8388624 | tf_op jit(solution)/shard_map/all_gather | solution.py:21
  394.9 8.1 %copy.24 = f32[8,8,64,512]{3,2,1,0:T(8,128)S(1)} copy(f32[8,8,64,512]{3,1,2,0:T(8,128)} %bitcast.292) | data formatting | bytes 16777216
  409.5 11.0 %all-reduce.7 = (f32[]{:T(128)}, f32[]{:T(128)}) all-reduce(f32[]{:T(128)S(6)} %add.196, f32[]{:T(128)S(6)} %add.197), channel_id=1, replica_groups=mesh['ord_0'=4,'ord_1'=4,'ord_2'=4,'rhs'=2] {'ord_0'}, use_global_device_ids=true, to_apply=%region_19.0 | all-reduce | flops 2 | bytes 16 | tf_op jit(solution)/shard_map/psum | solution.py:54
  420.5 11.1 %all-reduce.4 = (f32[]{:T(128)}, f32[]{:T(128)}) all-reduce(f32[]{:T(128)} %get-tuple-element.28, f32[]{:T(128)} %get-tuple-element.29), channel_id=1, replica_groups=mesh['ord_0'=4,'ord_1'=4,'ord_2'=4,'rhs'=2] {'ord_1'}, use_global_device_ids=true, to_apply=%region_20.0 | all-reduce | flops 2 | bytes 16 | tf_op jit(solution)/shard_map/psum | solution.py:54
  431.6 9.1 %all-reduce.1 = (f32[]{:T(128)}, f32[]{:T(128)}) all-reduce(f32[]{:T(128)} %get-tuple-element.22, f32[]{:T(128)} %get-tuple-element.23), channel_id=1, replica_groups=mesh['ord_0'=4,'ord_1'=4,'ord_2'=4,'rhs'=2] {'ord_2'}, use_global_device_ids=true, to_apply=%region_21.0 | all-reduce | flops 2 | bytes 16 | tf_op jit(solution)/shard_map/psum | solution.py:54
  444.9 5.6 convolution_multiply_fusion.1
  452.4 4.8 all-to-all-start.4
  457.4 9.7 %all-to-all-done.4 = f32[64,512,1]{1,2,0:T(1,128)S(1)} async-done(((f32[64,512,1]{1,2,0:T(1,128)}), f32[64,512,1]{1,2,0:T(1,128)S(1)}, u32[]{:S(2)}, u32[]{:S(2)}) %all-to-all-start.4) | async-done | bytes 131104 | tf_op jit(solution)/shard_map/all_to_all | solution.py:32
  468.2 14.6 %all_to_all.32 = f32[64,512,1]{1,2,0:T(1,128)S(1)} all-to-all(f32[64,512,1]{1,2,0:T(1,128)S(1)} %broadcast_in_dim.8), channel_id=1, replica_groups=mesh['ord_0'=4,'ord_1'=4,'ord_2'=4,'rhs'=2] {'ord_0','ord_1','ord_2'}, dimensions={0} | all-to-all | bytes 262144 | tf_op jit(solution)/shard_map/all_to_all | solution.py:44
  487.9 6.7 %fusion.85 = (bf16[8,64,640]{2,1,0:T(8,128)(2,1)S(1)}, f32[8,64,640]{2,1,0:T(8,128)}) fusion(f32[8,64,640]{2,1,0:T(8,128)S(1)} %copy-done.17, bf16[8,640,640]{2,1,0:T(8,128)(2,1)} %param.16, f32[8,640,64]{1,2,0:T(8,128)S(1)} %convolution_bitcast_fusion.1, f32[8,640]{1,0:T(8,128)S(1)} %fusion.63), kind=kOutput, calls=%fused_computation.144 | convolution fusion | flops 420741120 | bytes 11161600 | tf_op jit(solution)/shard_map/sij,sjc->sic/dot_general | solution.py:58
  497.2 4.4 convolution_bitcast_fusion
  513.8 60.9 %all-gather.15.cloned.1.call-done = f32[32768,64]{0,1:T(8,128)} async-done(((f32[512,64]{0,1:T(8,128)}), f32[32768,64]{0,1:T(8,128)}) %all-gather.15.cloned.1.call-update) | async-done | bytes 8388624 | tf_op jit(solution)/shard_map/all_gather | solution.py:21
  574.8 8.1 %copy.25 = f32[8,8,64,512]{3,2,1,0:T(8,128)S(1)} copy(f32[8,8,64,512]{3,1,2,0:T(8,128)} %bitcast.291) | data formatting | bytes 16777216
  588.9 10.9 %all-reduce.6 = (f32[]{:T(128)}, f32[]{:T(128)}) all-reduce(f32[]{:T(128)S(6)} %add.205, f32[]{:T(128)S(6)} %add.206), channel_id=1, replica_groups=mesh['ord_0'=4,'ord_1'=4,'ord_2'=4,'rhs'=2] {'ord_0'}, use_global_device_ids=true, to_apply=%region_33.0 | all-reduce | flops 2 | bytes 16 | tf_op jit(solution)/shard_map/psum | solution.py:54
  599.8 11.1 %all-reduce.3 = (f32[]{:T(128)}, f32[]{:T(128)}) all-reduce(f32[]{:T(128)} %get-tuple-element.26, f32[]{:T(128)} %get-tuple-element.27), channel_id=1, replica_groups=mesh['ord_0'=4,'ord_1'=4,'ord_2'=4,'rhs'=2] {'ord_1'}, use_global_device_ids=true, to_apply=%region_34.0 | all-reduce | flops 2 | bytes 16 | tf_op jit(solution)/shard_map/psum | solution.py:54
  610.9 9.1 %all-reduce = (f32[]{:T(128)}, f32[]{:T(128)}) all-reduce(f32[]{:T(128)} %get-tuple-element.20, f32[]{:T(128)} %get-tuple-element.21), channel_id=1, replica_groups=mesh['ord_0'=4,'ord_1'=4,'ord_2'=4,'rhs'=2] {'ord_2'}, use_global_device_ids=true, to_apply=%region_35.0 | all-reduce | flops 2 | bytes 16 | tf_op jit(solution)/shard_map/psum | solution.py:54
  (274 shorter events, 135.5 us)
Async XLA Ops:
  7.2 101.7 %copy-start = (f32[512,512]{1,0:T(8,128)S(1)}, f32[512,512]{1,0:T(8,128)}, u32[]{:S(2)}) copy-start(f32[512,512]{1,0:T(8,128)} %param.20) | copy-start | bytes 3145732
  7.2 90.5 %all-gather.9.cloned.1.call-start = ((), (), s32[]{:S(2)}) async-start(), calls=%async_computation.6 | async-start | bytes 8519680 | tf_op jit(solution)/shard_map/all_gather | solution.py:21
  9.4 19.2 %slice-start = ((s8[5242880]{0:T(1024)(128)(4,1)}), s8[1048576]{0:T(1024)(128)(4,1)S(1)}, s32[]{:S(2)}) async-start(s8[5242880]{0:T(1024)(128)(4,1)} %bitcast.251), calls=%async_computation.10 | async-start | bytes 2097152
  13.7 14.9 %slice-start.1 = ((s8[5242880]{0:T(1024)(128)(4,1)}), s8[4194304]{0:T(1024)(128)(4,1)S(1)}, s32[]{:S(2)}) async-start(s8[5242880]{0:T(1024)(128)(4,1)} %bitcast.251), calls=%async_computation.11 | async-start | bytes 8388608
  18.0 12.6 %collective-permute-start.1 = (bf16[1,640,64]{1,2,0:T(8,128)(2,1)S(1)}, bf16[1,640,64]{1,2,0:T(8,128)(2,1)S(1)}, u32[]{:S(2)}, u32[]{:S(2)}) collective-permute-start(bf16[1,640,64]{1,2,0:T(8,128)(2,1)S(1)} %slice.91), channel_id=1, source_target_pairs={{0,2},{2,4},{4,6},{6,8},{8,10},{10,12},{12,14},{14,16},{16,18},{18... | collective-permute-start | bytes 245768 | tf_op jit(solution)/shard_map/ppermute | solution.py:17
  21.9 8.6 %collective-permute-start = (bf16[1,640,64]{1,2,0:T(8,128)(2,1)S(1)}, bf16[1,640,64]{1,2,0:T(8,128)(2,1)S(1)}, u32[]{:S(2)}, u32[]{:S(2)}) collective-permute-start(bf16[1,640,64]{1,2,0:T(8,128)(2,1)S(1)} %slice.69), channel_id=1, source_target_pairs={{2,0},{4,2},{6,4},{8,6},{10,8},{12,10},{14,12},{16,14},{18,16},{20... | collective-permute-start | bytes 245768 | tf_op jit(solution)/shard_map/ppermute | solution.py:17
  38.0 22.7 %all-to-all-start = ((f32[64,512,1]{1,2,0:T(1,128)}), f32[64,512,1]{1,2,0:T(1,128)S(1)}, u32[]{:S(2)}, u32[]{:S(2)}) async-start(f32[64,512,1]{1,2,0:T(1,128)} %copy.13), calls=%async_computation | async-start | bytes 262144 | tf_op jit(solution)/shard_map/all_to_all | solution.py:32
  50.3 163.8 %all-gather.11.cloned.1.call-start = ((), (), s32[]{:S(2)}) async-start(), calls=%async_computation.7 | async-start | bytes 8519680 | tf_op jit(solution)/shard_map/all_gather | solution.py:21
  97.7 31.1 %slice-start.2 = ((s8[5242880]{0:T(1024)(128)(4,1)}), s8[4194304]{0:T(1024)(128)(4,1)S(1)}, s32[]{:S(2)}) async-start(s8[5242880]{0:T(1024)(128)(4,1)} %bitcast.253), calls=%async_computation.12 | async-start | bytes 8388608
  97.7 31.1 %slice-start.3 = ((s8[5242880]{0:T(1024)(128)(4,1)}), s8[1048576]{0:T(1024)(128)(4,1)S(1)}, s32[]{:S(2)}) async-start(s8[5242880]{0:T(1024)(128)(4,1)} %bitcast.253), calls=%async_computation.13 | async-start | bytes 2097152
  106.0 24.5 %slice-start.22 = ((s8[6553600]{0:T(1024)(128)(4,1)}), s8[4194304]{0:T(1024)(128)(4,1)S(1)}, s32[]{:S(2)}) async-start(s8[6553600]{0:T(1024)(128)(4,1)} %bitcast.273), calls=%async_computation.32 | async-start | bytes 8388608
  108.6 22.0 %slice-start.23 = ((s8[6553600]{0:T(1024)(128)(4,1)}), s8[2359296]{0:T(1024)(128)(4,1)S(1)}, s32[]{:S(2)}) async-start(s8[6553600]{0:T(1024)(128)(4,1)} %bitcast.273), calls=%async_computation.33 | async-start | bytes 4718592
  108.8 19.3 %copy-start.31 = (f32[512,64]{0,1:T(8,128)}, f32[512,64]{0,1:T(8,128)S(1)}, u32[]{:S(2)}) copy-start(f32[512,64]{0,1:T(8,128)S(1)} %fusion.23) | copy-start | bytes 393220
  136.4 9.1 %slice-start.26 = ((s8[6553600]{0:T(1024)(128)(4,1)}), s8[2359296]{0:T(1024)(128)(4,1)S(1)}, s32[]{:S(2)}) async-start(s8[6553600]{0:T(1024)(128)(4,1)} %bitcast.277), calls=%async_computation.36 | async-start | bytes 4718592
  136.4 9.0 %slice-start.27 = ((s8[6553600]{0:T(1024)(128)(4,1)}), s8[4194304]{0:T(1024)(128)(4,1)S(1)}, s32[]{:S(2)}) async-start(s8[6553600]{0:T(1024)(128)(4,1)} %bitcast.277), calls=%async_computation.37 | async-start | bytes 8388608
  140.9 7.0 %collective-permute-start.3 = (bf16[1,640,64]{1,2,0:T(8,128)(2,1)S(1)}, bf16[1,640,64]{1,2,0:T(8,128)(2,1)S(1)}, u32[]{:S(2)}, u32[]{:S(2)}) collective-permute-start(bf16[1,640,64]{1,2,0:T(8,128)(2,1)S(1)} %slice.90), channel_id=1, source_target_pairs={{0,2},{2,4},{4,6},{6,8},{8,10},{10,12},{12,14},{14,16},{16,18},{18... | collective-permute-start | bytes 245768 | tf_op jit(solution)/shard_map/ppermute | solution.py:17
  143.4 6.8 %collective-permute-start.2 = (bf16[1,640,64]{1,2,0:T(8,128)(2,1)S(1)}, bf16[1,640,64]{1,2,0:T(8,128)(2,1)S(1)}, u32[]{:S(2)}, u32[]{:S(2)}) collective-permute-start(bf16[1,640,64]{1,2,0:T(8,128)(2,1)S(1)} %slice.73), channel_id=1, source_target_pairs={{2,0},{4,2},{6,4},{8,6},{10,8},{12,10},{14,12},{16,14},{18,16},{20... | collective-permute-start | bytes 245768 | tf_op jit(solution)/shard_map/ppermute | solution.py:17
  271.6 39.8 %slice-start.24 = ((s8[6553600]{0:T(1024)(128)(4,1)}), s8[2359296]{0:T(1024)(128)(4,1)S(1)}, s32[]{:S(2)}) async-start(s8[6553600]{0:T(1024)(128)(4,1)} %bitcast.275), calls=%async_computation.34 | async-start | bytes 4718592
  273.5 15.3 %all-to-all-start.2 = ((f32[64,512,1]{1,2,0:T(1,128)}), f32[64,512,1]{1,2,0:T(1,128)}, u32[]{:S(2)}, u32[]{:S(2)}) async-start(f32[64,512,1]{1,2,0:T(1,128)} %copy.15), calls=%async_computation.2 | async-start | bytes 262144 | tf_op jit(solution)/shard_map/all_to_all | solution.py:32
  279.1 115.8 %all-gather.13.cloned.1.call-start = ((), (), s32[]{:S(2)}) async-start(), calls=%async_computation.8 | async-start | bytes 8519680 | tf_op jit(solution)/shard_map/all_gather | solution.py:21
  289.8 21.6 %slice-start.25 = ((s8[6553600]{0:T(1024)(128)(4,1)}), s8[4194304]{0:T(1024)(128)(4,1)S(1)}, s32[]{:S(2)}) async-start(s8[6553600]{0:T(1024)(128)(4,1)} %bitcast.275), calls=%async_computation.35 | async-start | bytes 8388608
  291.7 19.7 %copy-start.22 = (f32[8,64,640]{2,1,0:T(8,128)S(1)}, f32[8,64,640]{2,1,0:T(8,128)}, u32[]{:S(2)}) copy-start(f32[8,64,640]{2,1,0:T(8,128)} %copy-done.21) | copy-start | bytes 3932164
  321.8 6.5 %collective-permute-start.5 = (bf16[1,640,64]{1,2,0:T(8,128)(2,1)S(1)}, bf16[1,640,64]{1,2,0:T(8,128)(2,1)S(1)}, u32[]{:S(2)}, u32[]{:S(2)}) collective-permute-start(bf16[1,640,64]{1,2,0:T(8,128)(2,1)S(1)} %slice.89), channel_id=1, source_target_pairs={{0,2},{2,4},{4,6},{6,8},{8,10},{10,12},{12,14},{14,16},{16,18},{18... | collective-permute-start | bytes 245768 | tf_op jit(solution)/shard_map/ppermute | solution.py:17
  324.3 6.8 %collective-permute-start.4 = (bf16[1,640,64]{1,2,0:T(8,128)(2,1)S(1)}, bf16[1,640,64]{1,2,0:T(8,128)(2,1)S(1)}, u32[]{:S(2)}, u32[]{:S(2)}) collective-permute-start(bf16[1,640,64]{1,2,0:T(8,128)(2,1)S(1)} %slice.77), channel_id=1, source_target_pairs={{2,0},{4,2},{6,4},{8,6},{10,8},{12,10},{14,12},{16,14},{18,16},{20... | collective-permute-start | bytes 245768 | tf_op jit(solution)/shard_map/ppermute | solution.py:17
  403.1 47.4 %slice-start.8 = ((s8[5242880]{0:T(1024)(128)(4,1)}), s8[1048576]{0:T(1024)(128)(4,1)S(1)}, s32[]{:S(2)}) async-start(s8[5242880]{0:T(1024)(128)(4,1)} %bitcast.259), calls=%async_computation.18 | async-start | bytes 2097152
  452.4 14.6 %all-to-all-start.4 = ((f32[64,512,1]{1,2,0:T(1,128)}), f32[64,512,1]{1,2,0:T(1,128)S(1)}, u32[]{:S(2)}, u32[]{:S(2)}) async-start(f32[64,512,1]{1,2,0:T(1,128)} %copy.17), calls=%async_computation.4 | async-start | bytes 262144 | tf_op jit(solution)/shard_map/all_to_all | solution.py:32
  457.2 117.5 %all-gather.15.cloned.1.call-start = ((), (), s32[]{:S(2)}) async-start(), calls=%async_computation.9 | async-start | bytes 8519680 | tf_op jit(solution)/shard_map/all_gather | solution.py:21
  457.3 30.5 %copy-start.44 = (f32[512,64]{0,1:T(8,128)}, f32[512,64]{0,1:T(8,128)S(1)}, u32[]{:S(2)}) copy-start(f32[512,64]{0,1:T(8,128)S(1)} %multiply_subtract_fusion.3) | copy-start | bytes 393220
  483.5 12.0 %slice-start.10 = ((s8[5242880]{0:T(1024)(128)(4,1)}), s8[4194304]{0:T(1024)(128)(4,1)S(1)}, s32[]{:S(2)}) async-start(s8[5242880]{0:T(1024)(128)(4,1)} %bitcast.261), calls=%async_computation.20 | async-start | bytes 8388608
  501.6 6.6 %collective-permute-start.7 = (bf16[1,640,64]{1,2,0:T(8,128)(2,1)S(1)}, bf16[1,640,64]{1,2,0:T(8,128)(2,1)S(1)}, u32[]{:S(2)}, u32[]{:S(2)}) collective-permute-start(bf16[1,640,64]{1,2,0:T(8,128)(2,1)S(1)} %slice.88), channel_id=1, source_target_pairs={{0,2},{2,4},{4,6},{6,8},{8,10},{10,12},{12,14},{14,16},{16,18},{18... | collective-permute-start | bytes 245768 | tf_op jit(solution)/shard_map/ppermute | solution.py:17
  504.2 6.8 %collective-permute-start.6 = (bf16[1,640,64]{1,2,0:T(8,128)(2,1)S(1)}, bf16[1,640,64]{1,2,0:T(8,128)(2,1)S(1)}, u32[]{:S(2)}, u32[]{:S(2)}) collective-permute-start(bf16[1,640,64]{1,2,0:T(8,128)(2,1)S(1)} %slice.81), channel_id=1, source_target_pairs={{2,0},{4,2},{6,4},{8,6},{10,8},{12,10},{14,12},{16,14},{18,16},{20... | collective-permute-start | bytes 245768 | tf_op jit(solution)/shard_map/ppermute | solution.py:17
  582.9 41.5 %copy-start.27 = (f32[8,64,640]{2,1,0:T(8,128)S(1)}, f32[8,64,640]{2,1,0:T(8,128)}, u32[]{:S(2)}) copy-start(f32[8,64,640]{2,1,0:T(8,128)} %get-tuple-element.39) | copy-start | bytes 3932164
  (63 other events, 270.0 us)
Sparse Core Ops, SparseCore 0:
  13.9 83.7 all-gather.8
  136.5 77.4 all-gather.10
  317.4 77.4 all-gather.12
  497.3 77.4 all-gather.14
where the time goes:
time: 644 us; the launch traced here: 636 us
  waiting for transfers between devices  253 us (39%)
  blocking collectives  150 us (23%)
  matrix products  101 us (16%)
  local copies, waits for them, and re-layouts  42 us (7%)
  starting transfers between devices  41.1 us (6%)
  between operations  26.7 us (4%)
  other arithmetic  20.9 us (3%)
    all_gather x4, waiting for transfers between devices, total_of_pieces(): parts = lax.all_gather(array, axis)  217 us
    psum x12, blocking collectives, over_axes(): return functools.reduce(lax.psum, axes, array)  103 us
    dot_general x14, matrix products, batched(): jnp.einsum('sij,sjc->sic', matrices, vectors, preferred_element_type=jnp....  51.7 us
    all_to_all x3, blocking collectives, from_everyone(): lax.all_to_all(jnp.broadcast_to(array[None], (count, *array.shape)), axis...  47.5 us
    unnamed x164, local copies, waits for them, and re-layouts  38.8 us
    all_to_all x3, waiting for transfers between devices, summed_on_arrival(): parts = lax.all_to_all(cut_along(array, dim, count), axis, 0, 0, tiled=True)  27.8 us
    all_to_all x3, starting transfers between devices, summed_on_arrival(): parts = lax.all_to_all(cut_along(array, dim, count), axis, 0, 0, tiled=True)  22.7 us
    ppermute x8, starting transfers between devices, shifted(): lax.ppermute(value, axis, [(source, source + steps) for source in range(l...  18 us
  transfers between devices with their start and end apart: 15, of which 10 were waited for; matrix products, arithmetic and copies ran while one was open for 8% of the time, Pallas kernels for 0%

commit v1 on v0

v1 whole, which is shorter than its diff:
```python
import functools

import jax
import jax.numpy as jnp
from jax import lax
from jax.experimental import pallas as pl
from jax.experimental.pallas import tpu as pltpu
from jax.sharding import Mesh
from jax.sharding import PartitionSpec as P

ITERS = 3
AXES = ("ord_0", "ord_1", "ord_2")
F32, BF16 = jnp.float32, jnp.bfloat16
SIDE = 4
WIRE = (F32, F32, BF16, BF16)
MIB = 1 << 20


def nt(a, b):
    return lax.dot_general(a, b, (((1,), (1,)), ((), ())), preferred_element_type=F32)


def nn(a, b):
    return lax.dot_general(a, b, (((1,), (0,)), ((), ())), preferred_element_type=F32)


def nt_full(a, b):
    return lax.dot_general(
        a, b, (((1,), (1,)), ((), ())), precision=lax.Precision.HIGHEST, preferred_element_type=F32
    )


def two_parts(value):
    high = value.astype(BF16)
    low = (value - high.astype(F32)).astype(BF16)
    return jnp.concatenate([high, low], 0)


def nt_wide(value, b):
    rows = value.shape[0]
    both = nt(two_parts(value), b)
    return both[:rows] + both[rows:]


def live_row(counts, m, rows):
    return (lax.broadcasted_iota(jnp.int32, (1, rows), 1) < counts[m]).astype(F32)


def total(value):
    return jnp.sum(value, keepdims=True)


def call(kernel, outs, args, spaces, scratch=(), limit=16, flops=10**8):
    where = {"v": pltpu.VMEM, "m": pltpu.VMEM, "s": pltpu.SMEM}
    args = [
        pltpu.with_memory_space_constraint(a, pltpu.VMEM) if s == "m" else a
        for a, s in zip(args, spaces, strict=True)
    ]
    return pl.pallas_call(
        kernel,
        out_shape=[jax.ShapeDtypeStruct(*o) for o in outs],
        in_specs=[pl.BlockSpec(memory_space=where[s]) for s in spaces],
        out_specs=[pl.BlockSpec(memory_space=pltpu.VMEM)] * len(outs),
        scratch_shapes=list(scratch),
        compiler_params=pltpu.CompilerParams(vmem_limit_bytes=limit * MIB),
        cost_estimate=pl.CostEstimate(flops=flops, bytes_accessed=10**6, transcendentals=0),
    )(*args)


def tail_rows(dtype):
    return 8 if dtype == F32 else 16


def scalar_tile(num, den, dtype):
    row = lax.broadcasted_iota(jnp.int32, (tail_rows(dtype), 128), 0)
    if dtype == F32:
        return jnp.where(row == 0, num, jnp.where(row == 1, den, 0.0))
    num_high, den_high = num.astype(BF16).astype(F32), den.astype(BF16).astype(F32)
    parts = (num_high, num - num_high, den_high, den - den_high)
    tile = jnp.zeros((tail_rows(dtype), 128), F32)
    for i, part in enumerate(parts):
        tile = jnp.where(row == i, part, tile)
    return tile.astype(BF16)


def scalars_of(tile):
    if tile.shape[0] == 8:
        return tile[0:1], tile[1:2]
    return tile[0:1] + tile[1:2], tile[2:3] + tile[3:4]


def emit(me, sums, outs, num, den):
    share = sums[0].shape[0] // SIDE
    for k, out in enumerate(outs):
        first = pl.multiple_of(lax.rem(me + k, SIDE) * share, share)
        row = 0
        for chunk in range(sums[0].shape[1] // 128):
            for one in sums:
                out[row : row + share, :] = one[pl.ds(first, share), chunk * 128 : chunk * 128 + 128].astype(out.dtype)
                row += share
        out[row:, :] = scalar_tile(num, den, out.dtype)


def added(parts):
    p = [part[...].astype(F32) for part in parts]
    return (p[0] + p[2]) + (p[1] + p[3])


def sum_kernel(a, b, c, d, out):
    value = added((a, b, c, d))
    tail = tail_rows(out.dtype)
    out[:-tail, :] = value[:-tail].astype(out.dtype)
    num, den = scalars_of(value[-tail:])
    out[-tail:, :] = scalar_tile(num, den, out.dtype)


def combined(parts):
    first = parts[0]
    return call(sum_kernel, [(first.shape, first.dtype)], parts, "vvvv", limit=4, flops=10**5)[0]


def swapped(values, axis):
    got = [values[0]]
    for k in range(1, SIDE):
        got.append(lax.ppermute(values[k], axis, [(i, (i + k) % SIDE) for i in range(SIDE)]))
    return got


def reduced(shares):
    mine = combined(swapped(shares, AXES[0]))
    mine = combined(swapped([mine] * SIDE, AXES[1]))
    return swapped([mine] * SIDE, AXES[2])


def unpacked(value, count, chunks=4):
    tail = value.shape[0] % 32 or 16
    share = (value.shape[0] - tail) // (count * chunks)
    arrays = []
    for i in range(count):
        pieces = [value[(c * count + i) * share : (c * count + i + 1) * share] for c in range(chunks)]
        arrays.append(jnp.concatenate(pieces, 1))
    return arrays, scalars_of(value[-tail:])


def edge_start(counts, x, e, up, down):
    last = x.shape[0] - 1
    rows = x.shape[2]
    up[...] = (x[0] * live_row(counts, 0, rows)).astype(BF16)
    tail = (x[last] * live_row(counts, last, rows)).astype(BF16)
    down[...] = nn(tail, e[last]).astype(BF16)


def inner_start(counts, x, b, border, d, e, c, inv, r, y, edge, t, g, v):
    slots, _, rows = x.shape
    for m in range(slots):
        v[m] = (x[m] * live_row(counts, m, rows)).astype(BF16)
    narrow = border[...].astype(BF16)
    t[...] = jnp.zeros_like(t)
    g[...] = jnp.zeros_like(g)

    @pl.loop(1, slots - 1)
    def _(m):
        live = live_row(counts, m, rows)
        q = nt(v[m], d[m]) + nt(v[m + 1], e[m]) + nn(v[m - 1], e[m - 1]) + nt(narrow, c[m])
        res = live * (b[m] - q)
        blockwise = live * nt_wide(res, inv[m])
        r[m - 1] = res
        y[m - 1] = blockwise
        both = nn(jnp.concatenate([blockwise.astype(BF16), v[m]], 0), c[m])
        t[...] += both[: t.shape[0]]
        g[...] += both[t.shape[0] :]

    z = slots - 1
    edge[0] = nt(v[0], d[0]) + nt(v[1], e[0]) + nt(narrow, c[0])
    edge[1] = nt(v[z], d[z]) + nn(v[z - 1], e[z - 1]) + nt(narrow, c[z])


def outer_start(counts, me, x, b, edge, up, down, e, c, inv, t_in, g_in, r, y, s0, s1, s2, s3, t, g):
    slots, _, rows = x.shape
    z = slots - 1
    t[...] = t_in[...]
    g[...] = g_in[...]
    for i, m in enumerate((0, z)):
        live = live_row(counts, m, rows)
        other = down[...].astype(F32) if i == 0 else nt(up[...], e[z])
        res = live * (b[m] - (edge[i] + other))
        blockwise = live * nt_wide(res, inv[m])
        r[i] = res
        y[i] = blockwise
        v = (x[m] * live).astype(BF16)
        both = nn(jnp.concatenate([blockwise.astype(BF16), v], 0), c[m])
        t[...] += both[: t.shape[0]]
        g[...] += both[t.shape[0] :]
    zero = jnp.zeros((1, 1), F32)
    emit(me[0], (t, g), (s0, s1, s2, s3), zero, zero)


def border_start(me, p0, p1, p2, p3, rhs, border, bb, out, target):
    (s, g), _ = unpacked(added((p0, p1, p2, p3)), 2)
    share = s.shape[0]
    mine = pl.ds(pl.multiple_of(me[0] * share, share), share)
    left = rhs[mine, :] - nt(border[mine, :].astype(BF16), bb[...]) - g
    out[...] = left
    target[...] = left - s


def border_step(me, p0, p1, p2, p3, rb, wb, bb, out, diff, scal):
    arrays, (num, den) = unpacked(added((p0, p1, p2, p3)), 2 if diff is not None else 1)
    g = arrays[-1]
    share = g.shape[0]
    mine = pl.ds(pl.multiple_of(me[0] * share, share), share)
    q = nt(wb[mine, :].astype(BF16), bb[...]) + g
    out[...] = q
    if diff is not None:
        diff[...] = q - arrays[0]
    row = lax.broadcasted_iota(jnp.int32, scal.shape, 0)
    num = num * (1.0 / SIDE) + total(rb[...] * q)
    den = den * (1.0 / SIDE) + total(q * q)
    scal[...] = jnp.where(row == 0, num, jnp.where(row == 1, den, 0.0))


def border_last(me, p0, p1, p2, p3, rb, wb, bb, out, scal):
    border_step(me, p0, p1, p2, p3, rb, wb, bb, out, None, scal)


def solve(target, s, out):
    out[...] = nt_full(target[...], s[...])


def step_of(parts, border):
    tile = added([part.at[:, border : border + 128] for part in parts])
    return tile[0:1] / (tile[1:2] + 1e-06)


def place(me, parts, wb, scale, old):
    share = parts[0].shape[0]
    border = wb.shape[1]
    for k, part in enumerate(parts):
        rows = pl.ds(pl.multiple_of(lax.rem(me + SIDE - k, SIDE) * share, share), share)
        if old is None:
            wb[rows, :] = part[:, :border]
        else:
            wb[rows, :] = old[rows, :] + scale * part[:, :border]


def edge_update(counts, narrow, yv, c, inv, e, w, u, up, down, slots, rows):
    z = slots - 1
    for i, m in enumerate((0, z)):
        live = live_row(counts, m, rows)
        lift = nt(narrow, c[m])
        u[i] = lift
        value = yv[i] - live * nt(lift.astype(BF16), inv[m])
        w[i] = value
        if i == 0:
            up[...] = value.astype(BF16)
        else:
            down[...] = nn(value.astype(BF16), e[z]).astype(BF16)


def edge_first(counts, me, a0, a1, a2, a3, y, c, inv, e, wb, w, u, up, down):
    place(me[0], (a0, a1, a2, a3), wb, None, None)
    yv = [y[0], y[1]]
    edge_update(counts, wb[...].astype(BF16), yv, c, inv, e, w, u, up, down, inv.shape[0], inv.shape[1])


def edge_next(
    counts, me, a0, a1, a2, a3, wb_in, sol_in, rb_in, qb, y_in, p, r_in, q, c, inv, e,
    alpha, wb, sol, rb, y, r, w, u, up, down,
):
    parts = (a0, a1, a2, a3)
    border = wb.shape[1]
    step = step_of(parts, border)
    alpha[...] = jnp.broadcast_to(step, alpha.shape)
    a = step[:, :1]
    sol[...] = sol_in[...] + a * wb_in[...]
    place(me[0], parts, wb, -a, wb_in)
    rb[...] = rb_in[...] - a * qb[...]
    yv = []
    for i in range(2):
        r[i] = r_in[i] - a * q[i]
        value = y_in[i] - a * p[i]
        y[i] = value
        yv.append(value)
    edge_update(counts, wb[...].astype(BF16), yv, c, inv, e, w, u, up, down, inv.shape[0], inv.shape[1])


def inner_body(counts, load, narrow, w_edge, u_edge, d, e, c, inv, w, q, p, edge, t, g, num, den, v, u, keep):
    slots, rows, _ = inv.shape
    z = slots - 1
    v[0] = w_edge[0].astype(BF16)
    v[z] = w_edge[1].astype(BF16)

    @pl.loop(1, z)
    def _(m):
        live = live_row(counts, m, rows)
        lift = nt(narrow, c[m])
        u[m] = lift
        value = load(m) - live * nt(lift.astype(BF16), inv[m])
        w[m - 1] = value
        v[m] = value.astype(BF16)

    if t is not None:
        t[...] = jnp.zeros_like(t)
    g[...] = jnp.zeros_like(g)
    num[...] = jnp.zeros_like(num)
    den[...] = jnp.zeros_like(den)

    @pl.loop(1, z)
    def _(m):
        live = live_row(counts, m, rows)
        value = live * (nt(v[m], d[m]) + nt(v[m + 1], e[m]) + nn(v[m - 1], e[m - 1]) + u[m])
        num[...] += jnp.sum(keep(m) * value, 0, keepdims=True)
        den[...] += jnp.sum(value * value, 0, keepdims=True)
        if t is None:
            g[...] += nn(v[m], c[m])
        else:
            q[m - 1] = value
            back = live * nt_wide(value, inv[m])
            p[m - 1] = back
            both = nn(jnp.concatenate([back.astype(BF16), v[m]], 0), c[m])
            t[...] += both[: t.shape[0]]
            g[...] += both[t.shape[0] :]

    edge[0] = nt(v[0], d[0]) + nt(v[1], e[0]) + u_edge[0]
    edge[1] = nt(v[z], d[z]) + nn(v[z - 1], e[z - 1]) + u_edge[1]


def inner_first(counts, wb, w_edge, u_edge, y, r, d, e, c, inv, w, q, p, edge, t, g, num, den, v, u):
    inner_body(
        counts, lambda m: y[m - 1], wb[...].astype(BF16), w_edge, u_edge, d, e, c, inv,
        w, q, p, edge, t, g, num, den, v, u, lambda m: r[m - 1],
    )


def inner_next(
    counts, alpha, wb, w_edge, u_edge, y_in, p_in, r_in, q_in, d, e, c, inv,
    y, r, w, q, p, edge, t, g, num, den, v, u,
):
    a = alpha[0:1, 0:1]

    def load(m):
        y[m - 1] = y_in[m - 1] - a * p_in[m - 1]
        r[m - 1] = r_in[m - 1] - a * q_in[m - 1]
        return y[m - 1]

    inner_body(
        counts, load, wb[...].astype(BF16), w_edge, u_edge, d, e, c, inv,
        w, q, p, edge, t, g, num, den, v, u, lambda m: r[m - 1],
    )


def inner_last(
    counts, alpha, wb, w_edge, u_edge, y_in, p_in, r_in, q_in, d, e, c, inv,
    w, edge, g, num, den, v, u,
):
    a = alpha[0:1, 0:1]
    inner_body(
        counts, lambda m: y_in[m - 1] - a * p_in[m - 1], wb[...].astype(BF16), w_edge, u_edge, d, e, c, inv,
        w, None, None, edge, None, g, num, den, v, u, lambda m: r_in[m - 1] - a * q_in[m - 1],
    )


def outer_body(counts, me, w_edge, r_edge, edge, up, down, e, c, inv, t_in, g_in, num_in, den_in, q, p, shares, t, g):
    slots, rows, _ = inv.shape
    z = slots - 1
    if t is not None:
        t[...] = t_in[...]
    g[...] = g_in[...]
    num, den = total(num_in[...]), total(den_in[...])
    for i, m in enumerate((0, z)):
        live = live_row(counts, m, rows)
        other = down[...].astype(F32) if i == 0 else nt(up[...], e[z])
        value = live * (edge[i] + other)
        num += total(r_edge[i] * value)
        den += total(value * value)
        v = w_edge[i].astype(BF16)
        if t is None:
            g[...] += nn(v, c[m])
        else:
            q[i] = value
            back = live * nt_wide(value, inv[m])
            p[i] = back
            both = nn(jnp.concatenate([back.astype(BF16), v], 0), c[m])
            t[...] += both[: t.shape[0]]
            g[...] += both[t.shape[0] :]
    emit(me[0], (g,) if t is None else (t, g), shares, num, den)


def outer_step(counts, me, w_edge, r_edge, edge, up, down, e, c, inv, t_in, g_in, num, den, q, p, s0, s1, s2, s3, t, g):
    outer_body(
        counts, me, w_edge, r_edge, edge, up, down, e, c, inv, t_in, g_in, num, den, q, p, (s0, s1, s2, s3), t, g
    )


def outer_last(counts, me, w_edge, r_edge, edge, up, down, e, c, inv, g_in, num, den, s0, s1, s2, s3, g):
    outer_body(
        counts, me, w_edge, r_edge, edge, up, down, e, c, inv, None, g_in, num, den, None, None,
        (s0, s1, s2, s3), None, g,
    )


def finish(counts, a0, a1, a2, a3, wb, sol, x, al0, al1, e0, e1, e2, w0, w1, w2, out, border):
    slots, _, rows = x.shape
    step = step_of((a0, a1, a2, a3), 0)[:, :1]
    border[...] = sol[...] + step * wb[...]
    c0, c1 = al0[0:1, 0:1], al1[0:1, 0:1]
    for m in range(slots):
        if m in (0, slots - 1):
            i = 0 if m == 0 else 1
            a, b, c = e0[i], e1[i], e2[i]
        else:
            a, b, c = w0[m - 1], w1[m - 1], w2[m - 1]
        out[m] = ((x[m] * live_row(counts, m, rows) + c0 * a) + c1 * b) + step * c


def halo(up, down):
    count = lax.axis_size(AXES)
    ahead = lax.ppermute(up, AXES, [(i + 1, i) for i in range(count - 1)])
    behind = lax.ppermute(down, AXES, [(i, i + 1) for i in range(count - 1)])
    return ahead, behind


def shards(
    rhs_blocks, rhs_border, start_blocks, start_border,
    diag, inverse, coupling, border_coupling, border_block, schur, counts,
):
    x = start_blocks.transpose(0, 2, 1)
    b = rhs_blocks.transpose(0, 2, 1)
    border_rhs, border_x = rhs_border.T, start_border.T
    slots, columns, rows = x.shape
    border = border_x.shape[1]
    share = columns // SIDE
    me = lax.axis_index(AXES[0]).reshape(1).astype(jnp.int32)
    state, edges = ((slots - 2, columns, rows), F32), ((2, columns, rows), F32)
    one16, wide = ((columns, rows), BF16), ((columns, border), F32)
    line, piece = ((1, rows), F32), ((share, border), F32)
    tile = ((8, 128), F32)
    keep16 = pltpu.VMEM((slots, columns, rows), BF16)
    keep32 = pltpu.VMEM((slots, columns, rows), F32)
    acc = pltpu.VMEM((columns, border), F32)

    def message(dtype, sums):
        return ((share * sums * border // 128 + tail_rows(dtype), 128), dtype)

    up, down = call(edge_start, [one16, one16], [counts, x, coupling], "svm")
    up, down = halo(up, down)
    r, y, edge, t, g = call(
        inner_start,
        [state, state, edges, wide, wide],
        [counts, x, b, border_x, diag, coupling, border_coupling, inverse],
        "svvvmmmm",
        [keep16],
        flops=4 * 10**9,
    )
    r_edge, y_edge, *shares = call(
        outer_start,
        [edges, edges] + [message(WIRE[0], 2)] * SIDE,
        [counts, me, x, b, edge, up, down, coupling, border_coupling, inverse, t, g],
        "ssvvvvvmmmvv",
        [acc, acc],
        flops=5 * 10**8,
    )
    parts = reduced(shares)
    rb, target = call(
        border_start, [piece, piece], [me, *parts, border_rhs, border_x, border_block], "sv" + "v" * 6
    )
    found = call(solve, [piece], [target, schur], "vv")[0]
    gathered = swapped([found] * SIDE, AXES[0])

    steps, edge_updates, updates = [], [], []
    sol = border_x
    for k in range(ITERS):
        last = k == ITERS - 1
        if k == 0:
            wb, w_edge, u_edge, up, down = call(
                edge_first,
                [wide, edges, edges, one16, one16],
                [counts, me, *gathered, y_edge, border_coupling, inverse, coupling],
                "ssvvvvvmmm",
                flops=5 * 10**8,
            )
        else:
            step, wb, sol, rb, y_edge, r_edge, w_edge, u_edge, up, down = call(
                edge_next,
                [tile, wide, wide, piece, edges, edges, edges, edges, one16, one16],
                [counts, me, *gathered, wb, sol, rb, qb, y_edge, p_edge, r_edge, q_edge]
                + [border_coupling, inverse, coupling],
                "ss" + "v" * 12 + "mmm",
                flops=5 * 10**8,
            )
            steps.append(step)
        up, down = halo(up, down)
        matrices = [diag, coupling, border_coupling, inverse]
        if k == 0:
            w, q, p, edge, t, g, num, den = call(
                inner_first,
                [state, state, state, edges, wide, wide, line, line],
                [counts, wb, w_edge, u_edge, y, r] + matrices,
                "svvvvvmmmm",
                [keep16, keep32],
                flops=4 * 10**9,
            )
        elif not last:
            y, r, w, q, p, edge, t, g, num, den = call(
                inner_next,
                [state, state, state, state, state, edges, wide, wide, line, line],
                [counts, step, wb, w_edge, u_edge, y, p, r, q] + matrices,
                "s" + "v" * 8 + "mmmm",
                [keep16, keep32],
                limit=24,
                flops=4 * 10**9,
            )
        else:
            w, edge, g, num, den = call(
                inner_last,
                [state, edges, wide, line, line],
                [counts, step, wb, w_edge, u_edge, y, p, r, q] + matrices,
                "s" + "v" * 8 + "mmmm",
                [keep16, keep32],
                flops=3 * 10**9,
            )
        edge_updates.append(w_edge)
        updates.append(w)
        inputs = [counts, me, w_edge, r_edge, edge, up, down, coupling, border_coupling, inverse]
        if not last:
            q_edge, p_edge, *shares = call(
                outer_step,
                [edges, edges] + [message(WIRE[k + 1], 2)] * SIDE,
                inputs + [t, g, num, den],
                "ssvvvvvmmmvvvv",
                [acc, acc],
                flops=5 * 10**8,
            )
            parts = reduced(shares)
            qb, diff, scal = call(
                border_step,
                [piece, piece, ((share, 128), F32)],
                [me, *parts, rb, wb, border_block],
                "s" + "v" * 7,
            )
            partner = lax.ppermute(scal, "rhs", [(0, 1), (1, 0)])
            found = call(solve, [piece], [diff, schur], "vv")[0]
            sent = jnp.concatenate([found, scal + partner], 1)
        else:
            shares = call(
                outer_last,
                [message(WIRE[k + 1], 1)] * SIDE,
                inputs + [g, num, den],
                "ssvvvvvmmmvvv",
                [acc],
                flops=3 * 10**8,
            )
            parts = reduced(shares)
            qb, scal = call(
                border_last,
                [piece, ((share, 128), F32)],
                [me, *parts, rb, wb, border_block],
                "s" + "v" * 7,
            )
            partner = lax.ppermute(scal, "rhs", [(0, 1), (1, 0)])
            sent = scal + partner
        gathered = swapped([sent] * SIDE, AXES[0])
    out, border_out = call(
        finish,
        [(x.shape, F32), wide],
        [counts, *gathered, wb, sol, x, *steps, *edge_updates, *updates],
        "s" + "v" * 15,
        limit=24,
    )
    return out.transpose(0, 2, 1), border_out.T


def solution(mesh):
    finer = Mesh(mesh.devices.reshape(SIDE, SIDE, SIDE, mesh.shape["rhs"]), (*AXES, "rhs"))
    return jax.shard_map(
        shards,
        mesh=finer,
        in_specs=(
            P(AXES, None, "rhs"),
            P(None, "rhs"),
            P(AXES, None, "rhs"),
            P(None, "rhs"),
            P(AXES, None, None),
            P(AXES, None, None),
            P(AXES, None, None),
            P(AXES, None, None),
            P(),
            P(),
            P(AXES),
        ),
        out_specs=(P(AXES, None, "rhs"), P(None, "rhs")),
        check_vma=False,
    )
```

time: 644 us -> 283 us (0.44); the launches traced: 636 us -> 282 us
  waiting for transfers between devices: 253 us -> 68.8 us
  blocking collectives: 150 us -> 0 us
  matrix products: 101 us -> 0 us
  Pallas kernels: 0 us -> 71.4 us
  starting transfers between devices: 41.1 us -> 96.8 us
  between operations: 26.7 us -> 1.34 us
  other arithmetic: 20.9 us -> 0.03 us
    all_gather x4 -> x0, waiting for transfers between devices: 217 us -> none  [total_of_pieces(): parts = lax.all_gather(array, axis)]
    psum x12 -> x0, blocking collectives: 103 us -> none  [over_axes(): return functools.reduce(lax.psum, axes, array)]
    dot_general x36 -> x0, matrix products: 101 us -> none  [the longest x14 51.7 us: batched(): jnp.einsum('sij,sjc->sic', matrices, vectors, preferred_element_type=jnp....]
    ppermute x8 -> x59, starting transfers between devices: 18 us -> 96.8 us  [the longest x48 71.9 us: swapped(): lax.ppermute(values[k], axis, [(i, (i + k) % SIDE) for i in range(SIDE)])]
    pallas_call x0 -> x28, Pallas kernels: none -> 71.4 us  [call(): pl.pallas_call(kernel, out_shape=[jax.ShapeDtypeStruct(*o) for o in outs]...]
    ppermute x8 -> x59, waiting for transfers between devices: 7.87 us -> 68.8 us  [the longest x48 67.2 us: swapped(): lax.ppermute(values[k], axis, [(i, (i + k) % SIDE) for i in range(SIDE)])]
    all_to_all x3 -> x0, blocking collectives: 47.5 us -> none  [from_everyone(): lax.all_to_all(jnp.broadcast_to(array[None], (count, *array.shape)), axis...]
    all_to_all x3 -> x0, waiting for transfers between devices: 27.8 us -> none  [summed_on_arrival(): parts = lax.all_to_all(cut_along(array, dim, count), axis, 0, 0, tiled=True)]
  transfers between devices with their start and end apart: 15 -> 59, of which waited for: 10 -> 47; matrix products, arithmetic and copies ran while one was open for 8% -> 0% of each run, Pallas kernels for 0% -> 18%
where the time goes in v1:
time: 283 us; the launch traced here: 282 us
  starting transfers between devices  96.8 us (34%)
  Pallas kernels  71.4 us (25%)
  waiting for transfers between devices  68.8 us (24%)
  local copies, waits for them, and re-layouts  43.8 us (15%)
    ppermute x48, starting transfers between devices, swapped(): lax.ppermute(values[k], axis, [(i, (i + k) % SIDE) for i in range(SIDE)])  71.9 us
    pallas_call x28, Pallas kernels, call(): pl.pallas_call(kernel, out_shape=[jax.ShapeDtypeStruct(*o) for o in outs]...  71.4 us
    ppermute x48, waiting for transfers between devices, swapped(): lax.ppermute(values[k], axis, [(i, (i + k) % SIDE) for i in range(SIDE)])  67.2 us
    unnamed x114, local copies, waits for them, and re-layouts  43.8 us
    ppermute x4, starting transfers between devices, halo(): behind = lax.ppermute(down, AXES, [(i, i + 1) for i in range(count - 1)])  18.8 us
  transfers between devices with their start and end apart: 59, of which 47 were waited for; matrix products, arithmetic and copies ran while one was open for 0% of the time, Pallas kernels for 18%

profile of v1, /device:TPU:0, one launch (start us, length us, event | category | flops | bytes accessed | tf_op | source)
XLA Modules:
  0.0 282.2 jit_solution(7349443618602392826)
XLA Ops:
  8.4 5.2 %collective-permute-start.1 = (bf16[64,640]{1,0:T(8,128)(2,1)}, bf16[64,640]{1,0:T(8,128)(2,1)}, u32[]{:S(2)}, u32[]{:S(2)}) collective-permute-start(bf16[64,640]{1,0:T(8,128)(2,1)} %get-tuple-element.91), channel_id=1, source_target_pairs={{0,2},{2,4},{4,6},{6,8},{8,10},{10,12},{12,14},{14,16},{16,18},{18... | collective-permute-start | bytes 245768 | tf_op jit(solution)/shard_map/ppermute | solution.py:419
  13.7 2.9 %copy-done.4 = bf16[8,640,640]{2,1,0:T(8,128)(2,1)S(1)} copy-done((bf16[8,640,640]{2,1,0:T(8,128)(2,1)S(1)}, bf16[8,640,640]{2,1,0:T(8,128)(2,1)}, u32[]{:S(2)}) %copy-start.4) | copy-done | bytes 6553624
  19.0 2.9 %copy-done.11 = bf16[8,640,640]{2,1,0:T(8,128)(2,1)S(1)} copy-done((bf16[8,640,640]{2,1,0:T(8,128)(2,1)S(1)}, bf16[8,640,640]{2,1,0:T(8,128)(2,1)}, u32[]{:S(2)}) %copy-start.11) | copy-done | bytes 6553624
  22.8 10.8 %shard_map.122 = (f32[6,64,640]{2,1,0:T(8,128)S(1)}, f32[6,64,640]{2,1,0:T(8,128)S(1)}, f32[2,64,640]{2,1,0:T(8,128)S(1)}, f32[64,512]{1,0:T(8,128)S(1)}, f32[64,512]{1,0:T(8,128)S(1)}) custom-call(s32[8]{0:T(128)S(1)} %copy-done.45, f32[8,64,640]{2,1,0:T(8,128)S(1)} %bitcast.18, f32[8,64,640]{2,1,0:T(8,128)S(1)} %bitcast.21, f32[64,512]{1,0:T(8,128)S(1)} %bitcast.23, ...), custom_call_target="tpu_custom_call" | custom-call | flops 4000000000 | bytes 1000000 | tf_op jit(solution)/shard_map/pallas_call | solution.py:59
  35.9 3.2 %copy-done.2 = bf16[8,640,640]{2,1,0:T(8,128)(2,1)S(1)} copy-done((bf16[8,640,640]{2,1,0:T(8,128)(2,1)S(1)}, bf16[8,640,640]{2,1,0:T(8,128)(2,1)}, u32[]{:S(2)}) %copy-start.2) | copy-done | bytes 6553624
  39.1 2.9 %copy-done.5 = bf16[8,640,640]{2,1,0:T(8,128)(2,1)S(1)} copy-done((bf16[8,640,640]{2,1,0:T(8,128)(2,1)S(1)}, bf16[8,640,640]{2,1,0:T(8,128)(2,1)}, u32[]{:S(2)}) %copy-start.5) | copy-done | bytes 6553624
  51.4 5.5 %collective-permute-start.2 = (f32[136,128]{1,0:T(8,128)S(1)}, f32[136,128]{1,0:T(8,128)S(1)}, u32[]{:S(2)}, u32[]{:S(2)}) collective-permute-start(f32[136,128]{1,0:T(8,128)S(1)} %get-tuple-element.95), channel_id=1, source_target_pairs={{0,32},{32,64},{64,96},{96,0},{1,33},{33,65},{65,97},{97,1},{2,34}... | collective-permute-start | bytes 208904 | tf_op jit(solution)/shard_map/ppermute | solution.py:125
  56.9 3.0 %collective-permute-start.3 = (f32[136,128]{1,0:T(8,128)S(1)}, f32[136,128]{1,0:T(8,128)S(1)}, u32[]{:S(2)}, u32[]{:S(2)}) collective-permute-start(f32[136,128]{1,0:T(8,128)S(1)} %get-tuple-element.96), channel_id=1, source_target_pairs={{0,64},{32,96},{64,0},{96,32},{1,65},{33,97},{65,1},{97,33},{2,66}... | collective-permute-start | bytes 208904 | tf_op jit(solution)/shard_map/ppermute | solution.py:125
  71.4 4.9 %collective-permute-start.10 = (f32[136,128]{1,0:T(8,128)S(1)}, f32[136,128]{1,0:T(8,128)S(1)}, u32[]{:S(2)}, u32[]{:S(2)}) collective-permute-start(f32[136,128]{1,0:T(8,128)S(1)} %shard_map.126.p0), channel_id=1, source_target_pairs={{0,6},{2,0},{4,2},{6,4},{1,7},{3,1},{5,3},{7,5},{8,14},{10,8},{12,... | collective-permute-start | bytes 208904 | tf_op jit(solution)/shard_map/ppermute | solution.py:125
  78.9 3.3 %collective-permute-done.9.p2 = f32[136,128]{1,0:T(8,128)S(1)} collective-permute-done((f32[136,128]{1,0:T(8,128)S(1)}, f32[136,128]{1,0:T(8,128)S(1)}, u32[]{:S(2)}, u32[]{:S(2)}) %collective-permute-start.9) | collective-permute-done | bytes 69664 | tf_op jit(solution)/shard_map/ppermute | solution.py:125
  83.8 3.6 %collective-permute-start.13 = (f32[16,512]{1,0:T(8,128)S(1)}, f32[16,512]{1,0:T(8,128)S(1)}, u32[]{:S(2)}, u32[]{:S(2)}) collective-permute-start(f32[16,512]{1,0:T(8,128)S(1)} %shard_map.128.a0), channel_id=1, source_target_pairs={{0,96},{32,0},{64,32},{96,64},{1,97},{33,1},{65,33},{97,65},{2,98}... | collective-permute-start | bytes 98312 | tf_op jit(solution)/shard_map/ppermute | solution.py:125
  89.0 3.9 %collective-permute-done.12.a2 = f32[16,512]{1,0:T(8,128)S(1)} collective-permute-done((f32[16,512]{1,0:T(8,128)S(1)}, f32[16,512]{1,0:T(8,128)S(1)}, u32[]{:S(2)}, u32[]{:S(2)}) %collective-permute-start.12) | collective-permute-done | bytes 32800 | tf_op jit(solution)/shard_map/ppermute | solution.py:125
  92.9 2.9 %copy-done.3 = bf16[8,640,640]{2,1,0:T(8,128)(2,1)S(1)} copy-done((bf16[8,640,640]{2,1,0:T(8,128)(2,1)S(1)}, bf16[8,640,640]{2,1,0:T(8,128)(2,1)}, u32[]{:S(2)}) %copy-start.3) | copy-done | bytes 6553624
  98.8 4.6 %collective-permute-start.15 = (bf16[64,640]{1,0:T(8,128)(2,1)S(1)}, bf16[64,640]{1,0:T(8,128)(2,1)S(1)}, u32[]{:S(2)}, u32[]{:S(2)}) collective-permute-start(bf16[64,640]{1,0:T(8,128)(2,1)S(1)} %get-tuple-element.108), channel_id=1, source_target_pairs={{0,2},{2,4},{4,6},{6,8},{8,10},{10,12},{12,14},{14,16},{16,18},{18... | collective-permute-start | bytes 245768 | tf_op jit(solution)/shard_map/ppermute | solution.py:419
  106.3 13.0 %shard_map.130 = (f32[6,64,640]{2,1,0:T(8,128)S(1)}, f32[6,64,640]{2,1,0:T(8,128)S(1)}, f32[6,64,640]{2,1,0:T(8,128)S(1)}, f32[2,64,640]{2,1,0:T(8,128)S(1)}, f3...) custom-call(s32[8]{0:T(128)S(1)} %copy-done.46, ...), custom_call_target="tpu_custom_call" | custom-call | flops 4000000000 | bytes 1000000 | tf_op jit(solution)/shard_map/pallas_call | solution.py:59
  136.4 4.4 %collective-permute-start.24 = (f32[136,128]{1,0:T(8,128)S(1)}, f32[136,128]{1,0:T(8,128)S(1)}, u32[]{:S(2)}, u32[]{:S(2)}) collective-permute-start(f32[136,128]{1,0:T(8,128)S(1)} %shard_map.133.p0), channel_id=1, source_target_pairs={{0,6},{2,0},{4,2},{6,4},{1,7},{3,1},{5,3},{7,5},{8,14},{10,8},{12,... | collective-permute-start | bytes 208904 | tf_op jit(solution)/shard_map/ppermute | solution.py:125
  143.4 3.3 %collective-permute-done.23.p2 = f32[136,128]{1,0:T(8,128)S(1)} collective-permute-done((f32[136,128]{1,0:T(8,128)S(1)}, f32[136,128]{1,0:T(8,128)S(1)}, u32[]{:S(2)}, u32[]{:S(2)}) %collective-permute-start.23) | collective-permute-done | bytes 69664 | tf_op jit(solution)/shard_map/ppermute | solution.py:125
  148.7 3.0 %collective-permute-start.28 = (f32[16,640]{1,0:T(8,128)S(1)}, f32[16,640]{1,0:T(8,128)S(1)}, u32[]{:S(2)}, u32[]{:S(2)}) collective-permute-start(f32[16,640]{1,0:T(8,128)S(1)} %pad_maximum_fusion.a0), channel_id=1, source_target_pairs={{0,96},{32,0},{64,32},{96,64},{1,97},{33,1},{65,33},{97,65},{2,98}... | collective-permute-start | bytes 122888 | tf_op jit(solution)/shard_map/ppermute | solution.py:125
  153.9 3.3 %collective-permute-done.27.a2 = f32[16,640]{1,0:T(8,128)S(1)} collective-permute-done((f32[16,640]{1,0:T(8,128)S(1)}, f32[16,640]{1,0:T(8,128)S(1)}, u32[]{:S(2)}, u32[]{:S(2)}) %collective-permute-start.27) | collective-permute-done | bytes 40992 | tf_op jit(solution)/shard_map/ppermute | solution.py:125
  161.4 4.5 %collective-permute-start.30 = (bf16[64,640]{1,0:T(8,128)(2,1)}, bf16[64,640]{1,0:T(8,128)(2,1)S(1)}, u32[]{:S(2)}, u32[]{:S(2)}) collective-permute-start(bf16[64,640]{1,0:T(8,128)(2,1)} %get-tuple-element.132), channel_id=1, source_target_pairs={{0,2},{2,4},{4,6},{6,8},{8,10},{10,12},{12,14},{14,16},{16,18},{18... | collective-permute-start | bytes 245768 | tf_op jit(solution)/shard_map/ppermute | solution.py:419
  171.3 2.9 %copy-done.13 = bf16[8,640,640]{2,1,0:T(8,128)(2,1)S(1)} copy-done((bf16[8,640,640]{2,1,0:T(8,128)(2,1)S(1)}, bf16[8,640,640]{2,1,0:T(8,128)(2,1)}, u32[]{:S(2)}) %copy-start.13) | copy-done | bytes 6553624
  174.2 14.8 %shard_map.137 = (f32[6,64,640]{2,1,0:T(8,128)S(1)}, f32[6,64,640]{2,1,0:T(8,128)S(1)}, f32[6,64,640]{2,1,0:T(8,128)S(1)}, f32[6,64,640]{2,1,0:T(8,128)S(1)}, f3...) custom-call(s32[8]{0:T(128)S(1)} %copy-done.46, ...), custom_call_target="tpu_custom_call" | custom-call | flops 4000000000 | bytes 1000000 | tf_op jit(solution)/shard_map/pallas_call | solution.py:59
  205.6 4.0 %collective-permute-start.39 = (bf16[144,128]{1,0:T(8,128)(2,1)S(1)}, bf16[144,128]{1,0:T(8,128)(2,1)S(1)}, u32[]{:S(2)}, u32[]{:S(2)}) collective-permute-start(bf16[144,128]{1,0:T(8,128)(2,1)S(1)} %shard_map.140.p0), channel_id=1, source_target_pairs={{0,6},{2,0},{4,2},{6,4},{1,7},{3,1},{5,3},{7,5},{8,14},{10,8},{12,... | collective-permute-start | bytes 110600 | tf_op jit(solution)/shard_map/ppermute | solution.py:125
  211.2 3.9 %collective-permute-done.38.p2 = bf16[144,128]{1,0:T(8,128)(2,1)S(1)} collective-permute-done((bf16[144,128]{1,0:T(8,128)(2,1)S(1)}, bf16[144,128]{1,0:T(8,128)(2,1)S(1)}, u32[]{:S(2)}, u32[]{:S(2)}) %collective-permute-start.38) | collective-permute-done | bytes 36896 | tf_op jit(solution)/shard_map/ppermute | solution.py:125
  217.0 3.0 %collective-permute-start.43 = (f32[16,640]{1,0:T(8,128)S(1)}, f32[16,640]{1,0:T(8,128)S(1)}, u32[]{:S(2)}, u32[]{:S(2)}) collective-permute-start(f32[16,640]{1,0:T(8,128)S(1)} %pad_maximum_fusion.1.a0), channel_id=1, source_target_pairs={{0,96},{32,0},{64,32},{96,64},{1,97},{33,1},{65,33},{97,65},{2,98}... | collective-permute-start | bytes 122888 | tf_op jit(solution)/shard_map/ppermute | solution.py:125
  222.2 3.3 %collective-permute-done.42.a2 = f32[16,640]{1,0:T(8,128)S(1)} collective-permute-done((f32[16,640]{1,0:T(8,128)S(1)}, f32[16,640]{1,0:T(8,128)S(1)}, u32[]{:S(2)}, u32[]{:S(2)}) %collective-permute-start.42) | collective-permute-done | bytes 40992 | tf_op jit(solution)/shard_map/ppermute | solution.py:125
  229.9 4.6 %collective-permute-start.45 = (bf16[64,640]{1,0:T(8,128)(2,1)S(1)}, bf16[64,640]{1,0:T(8,128)(2,1)S(1)}, u32[]{:S(2)}, u32[]{:S(2)}) collective-permute-start(bf16[64,640]{1,0:T(8,128)(2,1)S(1)} %get-tuple-element.160), channel_id=1, source_target_pairs={{0,2},{2,4},{4,6},{6,8},{8,10},{10,12},{12,14},{14,16},{16,18},{18... | collective-permute-start | bytes 245768 | tf_op jit(solution)/shard_map/ppermute | solution.py:419
  234.6 10.5 %shard_map.144 = (f32[6,64,640]{2,1,0:T(8,128)S(1)}, f32[2,64,640]{2,1,0:T(8,128)S(1)}, f32[64,512]{1,0:T(8,128)S(1)}, f32[1,640]{1,0:T(1,128)S(1)}, f32[1,640]{1,0:T(1,128)S(1)}) custom-call(s32[8]{0:T(128)S(1)} %copy-done.46, f32[8,128]{1,0:T(8,128)S(1)} %get-tuple-element.151.alpha.al1, f32[64,512]{1,0:T(8,128)S(1)} %get-tuple-element.152.wb, ...), custom_call_target="tpu_custom_call" | custom-call | flops 3000000000 | bytes 1000000 | tf_op jit(solution)/shard_map/pallas_call | solution.py:59
  260.0 3.9 %collective-permute-start.54 = (bf16[80,128]{1,0:T(8,128)(2,1)S(1)}, bf16[80,128]{1,0:T(8,128)(2,1)S(1)}, u32[]{:S(2)}, u32[]{:S(2)}) collective-permute-start(bf16[80,128]{1,0:T(8,128)(2,1)S(1)} %shard_map.147.p0), channel_id=1, source_target_pairs={{0,6},{2,0},{4,2},{6,4},{1,7},{3,1},{5,3},{7,5},{8,14},{10,8},{12,... | collective-permute-start | bytes 61448 | tf_op jit(solution)/shard_map/ppermute | solution.py:125
  265.4 3.8 %collective-permute-done.53.p2 = bf16[80,128]{1,0:T(8,128)(2,1)S(1)} collective-permute-done((bf16[80,128]{1,0:T(8,128)(2,1)S(1)}, bf16[80,128]{1,0:T(8,128)(2,1)S(1)}, u32[]{:S(2)}, u32[]{:S(2)}) %collective-permute-start.53) | collective-permute-done | bytes 20512 | tf_op jit(solution)/shard_map/ppermute | solution.py:125
  271.3 3.1 %collective-permute-start.58 = (f32[16,128]{1,0:T(8,128)S(1)}, f32[16,128]{1,0:T(8,128)S(1)}, u32[]{:S(2)}, u32[]{:S(2)}) collective-permute-start(f32[16,128]{1,0:T(8,128)S(1)} %add.11.a0), channel_id=1, source_target_pairs={{0,96},{32,0},{64,32},{96,64},{1,97},{33,1},{65,33},{97,65},{2,98}... | collective-permute-start | bytes 24584 | tf_op jit(solution)/shard_map/ppermute | solution.py:125
  275.8 3.8 %collective-permute-done.57.a2 = f32[16,128]{1,0:T(8,128)S(1)} collective-permute-done((f32[16,128]{1,0:T(8,128)S(1)}, f32[16,128]{1,0:T(8,128)S(1)}, u32[]{:S(2)}, u32[]{:S(2)}) %collective-permute-start.57) | collective-permute-done | bytes 8224 | tf_op jit(solution)/shard_map/ppermute | solution.py:125
  (238 shorter events, 128.2 us)
Async XLA Ops:
  6.9 29.0 %collective-permute-start = (bf16[64,640]{1,0:T(8,128)(2,1)}, bf16[64,640]{1,0:T(8,128)(2,1)}, u32[]{:S(2)}, u32[]{:S(2)}) collective-permute-start(bf16[64,640]{1,0:T(8,128)(2,1)} %get-tuple-element.90), channel_id=1, source_target_pairs={{2,0},{4,2},{6,4},{8,6},{10,8},{12,10},{14,12},{16,14},{18,16},{20... | collective-permute-start | bytes 245768 | tf_op jit(solution)/shard_map/ppermute | solution.py:418
  8.4 27.5 %collective-permute-start.1 = (bf16[64,640]{1,0:T(8,128)(2,1)}, bf16[64,640]{1,0:T(8,128)(2,1)}, u32[]{:S(2)}, u32[]{:S(2)}) collective-permute-start(bf16[64,640]{1,0:T(8,128)(2,1)} %get-tuple-element.91), channel_id=1, source_target_pairs={{0,2},{2,4},{4,6},{6,8},{8,10},{10,12},{12,14},{14,16},{16,18},{18... | collective-permute-start | bytes 245768 | tf_op jit(solution)/shard_map/ppermute | solution.py:419
  51.4 9.7 %collective-permute-start.2 = (f32[136,128]{1,0:T(8,128)S(1)}, f32[136,128]{1,0:T(8,128)S(1)}, u32[]{:S(2)}, u32[]{:S(2)}) collective-permute-start(f32[136,128]{1,0:T(8,128)S(1)} %get-tuple-element.95), channel_id=1, source_target_pairs={{0,32},{32,64},{64,96},{96,0},{1,33},{33,65},{65,97},{97,1},{2,34}... | collective-permute-start | bytes 208904 | tf_op jit(solution)/shard_map/ppermute | solution.py:125
  56.9 6.1 %collective-permute-start.3 = (f32[136,128]{1,0:T(8,128)S(1)}, f32[136,128]{1,0:T(8,128)S(1)}, u32[]{:S(2)}, u32[]{:S(2)}) collective-permute-start(f32[136,128]{1,0:T(8,128)S(1)} %get-tuple-element.96), channel_id=1, source_target_pairs={{0,64},{32,96},{64,0},{96,32},{1,65},{33,97},{65,1},{97,33},{2,66}... | collective-permute-start | bytes 208904 | tf_op jit(solution)/shard_map/ppermute | solution.py:125
  64.8 5.8 %collective-permute-start.6 = (f32[136,128]{1,0:T(8,128)S(1)}, f32[136,128]{1,0:T(8,128)S(1)}, u32[]{:S(2)}, u32[]{:S(2)}) collective-permute-start(f32[136,128]{1,0:T(8,128)S(1)} %shard_map.125.a), channel_id=1, source_target_pairs={{0,16},{8,24},{16,0},{24,8},{1,17},{9,25},{17,1},{25,9},{2,18},{10... | collective-permute-start | bytes 208904 | tf_op jit(solution)/shard_map/ppermute | solution.py:125
  65.2 6.2 %collective-permute-start.5 = (f32[136,128]{1,0:T(8,128)S(1)}, f32[136,128]{1,0:T(8,128)S(1)}, u32[]{:S(2)}, u32[]{:S(2)}) collective-permute-start(f32[136,128]{1,0:T(8,128)S(1)} %shard_map.125.a), channel_id=1, source_target_pairs={{0,8},{8,16},{16,24},{24,0},{1,9},{9,17},{17,25},{25,1},{2,10},{10... | collective-permute-start | bytes 208904 | tf_op jit(solution)/shard_map/ppermute | solution.py:125
  71.4 7.5 %collective-permute-start.10 = (f32[136,128]{1,0:T(8,128)S(1)}, f32[136,128]{1,0:T(8,128)S(1)}, u32[]{:S(2)}, u32[]{:S(2)}) collective-permute-start(f32[136,128]{1,0:T(8,128)S(1)} %shard_map.126.p0), channel_id=1, source_target_pairs={{0,6},{2,0},{4,2},{6,4},{1,7},{3,1},{5,3},{7,5},{8,14},{10,8},{12,... | collective-permute-start | bytes 208904 | tf_op jit(solution)/shard_map/ppermute | solution.py:125
  76.3 5.9 %collective-permute-start.9 = (f32[136,128]{1,0:T(8,128)S(1)}, f32[136,128]{1,0:T(8,128)S(1)}, u32[]{:S(2)}, u32[]{:S(2)}) collective-permute-start(f32[136,128]{1,0:T(8,128)S(1)} %shard_map.126.p0), channel_id=1, source_target_pairs={{0,4},{2,6},{4,0},{6,2},{1,5},{3,7},{5,1},{7,3},{8,12},{10,14},{12... | collective-permute-start | bytes 208904 | tf_op jit(solution)/shard_map/ppermute | solution.py:125
  76.3 6.3 %collective-permute-start.8 = (f32[136,128]{1,0:T(8,128)S(1)}, f32[136,128]{1,0:T(8,128)S(1)}, u32[]{:S(2)}, u32[]{:S(2)}) collective-permute-start(f32[136,128]{1,0:T(8,128)S(1)} %shard_map.126.p0), channel_id=1, source_target_pairs={{0,2},{2,4},{4,6},{6,0},{1,3},{3,5},{5,7},{7,1},{8,10},{10,12},{12... | collective-permute-start | bytes 208904 | tf_op jit(solution)/shard_map/ppermute | solution.py:125
  87.4 5.5 %collective-permute-start.12 = (f32[16,512]{1,0:T(8,128)S(1)}, f32[16,512]{1,0:T(8,128)S(1)}, u32[]{:S(2)}, u32[]{:S(2)}) collective-permute-start(f32[16,512]{1,0:T(8,128)S(1)} %shard_map.128.a0), channel_id=1, source_target_pairs={{0,64},{32,96},{64,0},{96,32},{1,65},{33,97},{65,1},{97,33},{2,66}... | collective-permute-start | bytes 98312 | tf_op jit(solution)/shard_map/ppermute | solution.py:125
  87.4 5.5 %collective-permute-start.11 = (f32[16,512]{1,0:T(8,128)S(1)}, f32[16,512]{1,0:T(8,128)S(1)}, u32[]{:S(2)}, u32[]{:S(2)}) collective-permute-start(f32[16,512]{1,0:T(8,128)S(1)} %shard_map.128.a0), channel_id=1, source_target_pairs={{0,32},{32,64},{64,96},{96,0},{1,33},{33,65},{65,97},{97,1},{2,34}... | collective-permute-start | bytes 98312 | tf_op jit(solution)/shard_map/ppermute | solution.py:125
  97.5 21.8 %collective-permute-start.14 = (bf16[64,640]{1,0:T(8,128)(2,1)S(1)}, bf16[64,640]{1,0:T(8,128)(2,1)S(1)}, u32[]{:S(2)}, u32[]{:S(2)}) collective-permute-start(bf16[64,640]{1,0:T(8,128)(2,1)S(1)} %get-tuple-element.107), channel_id=1, source_target_pairs={{2,0},{4,2},{6,4},{8,6},{10,8},{12,10},{14,12},{16,14},{18,16},{20... | collective-permute-start | bytes 245768 | tf_op jit(solution)/shard_map/ppermute | solution.py:418
  98.8 20.5 %collective-permute-start.15 = (bf16[64,640]{1,0:T(8,128)(2,1)S(1)}, bf16[64,640]{1,0:T(8,128)(2,1)S(1)}, u32[]{:S(2)}, u32[]{:S(2)}) collective-permute-start(bf16[64,640]{1,0:T(8,128)(2,1)S(1)} %get-tuple-element.108), channel_id=1, source_target_pairs={{0,2},{2,4},{4,6},{6,8},{8,10},{10,12},{12,14},{14,16},{16,18},{18... | collective-permute-start | bytes 245768 | tf_op jit(solution)/shard_map/ppermute | solution.py:419
  121.2 5.6 %collective-permute-start.16 = (f32[136,128]{1,0:T(8,128)S(1)}, f32[136,128]{1,0:T(8,128)S(1)}, u32[]{:S(2)}, u32[]{:S(2)}) collective-permute-start(f32[136,128]{1,0:T(8,128)S(1)} %get-tuple-element.114), channel_id=1, source_target_pairs={{0,32},{32,64},{64,96},{96,0},{1,33},{33,65},{65,97},{97,1},{2,34}... | collective-permute-start | bytes 208904 | tf_op jit(solution)/shard_map/ppermute | solution.py:125
  121.9 5.8 %collective-permute-start.17 = (f32[136,128]{1,0:T(8,128)S(1)}, f32[136,128]{1,0:T(8,128)S(1)}, u32[]{:S(2)}, u32[]{:S(2)}) collective-permute-start(f32[136,128]{1,0:T(8,128)S(1)} %get-tuple-element.115), channel_id=1, source_target_pairs={{0,64},{32,96},{64,0},{96,32},{1,65},{33,97},{65,1},{97,33},{2,66}... | collective-permute-start | bytes 208904 | tf_op jit(solution)/shard_map/ppermute | solution.py:125
  129.3 5.8 %collective-permute-start.20 = (f32[136,128]{1,0:T(8,128)S(1)}, f32[136,128]{1,0:T(8,128)S(1)}, u32[]{:S(2)}, u32[]{:S(2)}) collective-permute-start(f32[136,128]{1,0:T(8,128)S(1)} %shard_map.132.a), channel_id=1, source_target_pairs={{0,16},{8,24},{16,0},{24,8},{1,17},{9,25},{17,1},{25,9},{2,18},{10... | collective-permute-start | bytes 208904 | tf_op jit(solution)/shard_map/ppermute | solution.py:125
  130.9 5.5 %collective-permute-start.19 = (f32[136,128]{1,0:T(8,128)S(1)}, f32[136,128]{1,0:T(8,128)S(1)}, u32[]{:S(2)}, u32[]{:S(2)}) collective-permute-start(f32[136,128]{1,0:T(8,128)S(1)} %shard_map.132.a), channel_id=1, source_target_pairs={{0,8},{8,16},{16,24},{24,0},{1,9},{9,17},{17,25},{25,1},{2,10},{10... | collective-permute-start | bytes 208904 | tf_op jit(solution)/shard_map/ppermute | solution.py:125
  136.4 7.0 %collective-permute-start.24 = (f32[136,128]{1,0:T(8,128)S(1)}, f32[136,128]{1,0:T(8,128)S(1)}, u32[]{:S(2)}, u32[]{:S(2)}) collective-permute-start(f32[136,128]{1,0:T(8,128)S(1)} %shard_map.133.p0), channel_id=1, source_target_pairs={{0,6},{2,0},{4,2},{6,4},{1,7},{3,1},{5,3},{7,5},{8,14},{10,8},{12,... | collective-permute-start | bytes 208904 | tf_op jit(solution)/shard_map/ppermute | solution.py:125
  140.8 5.9 %collective-permute-start.23 = (f32[136,128]{1,0:T(8,128)S(1)}, f32[136,128]{1,0:T(8,128)S(1)}, u32[]{:S(2)}, u32[]{:S(2)}) collective-permute-start(f32[136,128]{1,0:T(8,128)S(1)} %shard_map.133.p0), channel_id=1, source_target_pairs={{0,4},{2,6},{4,0},{6,2},{1,5},{3,7},{5,1},{7,3},{8,12},{10,14},{12... | collective-permute-start | bytes 208904 | tf_op jit(solution)/shard_map/ppermute | solution.py:125
  140.8 6.3 %collective-permute-start.22 = (f32[136,128]{1,0:T(8,128)S(1)}, f32[136,128]{1,0:T(8,128)S(1)}, u32[]{:S(2)}, u32[]{:S(2)}) collective-permute-start(f32[136,128]{1,0:T(8,128)S(1)} %shard_map.133.p0), channel_id=1, source_target_pairs={{0,2},{2,4},{4,6},{6,0},{1,3},{3,5},{5,7},{7,1},{8,10},{10,12},{12... | collective-permute-start | bytes 208904 | tf_op jit(solution)/shard_map/ppermute | solution.py:125
  151.7 5.5 %collective-permute-start.27 = (f32[16,640]{1,0:T(8,128)S(1)}, f32[16,640]{1,0:T(8,128)S(1)}, u32[]{:S(2)}, u32[]{:S(2)}) collective-permute-start(f32[16,640]{1,0:T(8,128)S(1)} %pad_maximum_fusion.a0), channel_id=1, source_target_pairs={{0,64},{32,96},{64,0},{96,32},{1,65},{33,97},{65,1},{97,33},{2,66}... | collective-permute-start | bytes 122888 | tf_op jit(solution)/shard_map/ppermute | solution.py:125
  152.1 5.5 %collective-permute-start.26 = (f32[16,640]{1,0:T(8,128)S(1)}, f32[16,640]{1,0:T(8,128)S(1)}, u32[]{:S(2)}, u32[]{:S(2)}) collective-permute-start(f32[16,640]{1,0:T(8,128)S(1)} %pad_maximum_fusion.a0), channel_id=1, source_target_pairs={{0,32},{32,64},{64,96},{96,0},{1,33},{33,65},{65,97},{97,1},{2,34}... | collective-permute-start | bytes 122888 | tf_op jit(solution)/shard_map/ppermute | solution.py:125
  160.1 28.9 %collective-permute-start.29 = (bf16[64,640]{1,0:T(8,128)(2,1)}, bf16[64,640]{1,0:T(8,128)(2,1)S(1)}, u32[]{:S(2)}, u32[]{:S(2)}) collective-permute-start(bf16[64,640]{1,0:T(8,128)(2,1)} %get-tuple-element.131), channel_id=1, source_target_pairs={{2,0},{4,2},{6,4},{8,6},{10,8},{12,10},{14,12},{16,14},{18,16},{20... | collective-permute-start | bytes 245768 | tf_op jit(solution)/shard_map/ppermute | solution.py:418
  161.4 27.6 %collective-permute-start.30 = (bf16[64,640]{1,0:T(8,128)(2,1)}, bf16[64,640]{1,0:T(8,128)(2,1)S(1)}, u32[]{:S(2)}, u32[]{:S(2)}) collective-permute-start(bf16[64,640]{1,0:T(8,128)(2,1)} %get-tuple-element.132), channel_id=1, source_target_pairs={{0,2},{2,4},{4,6},{6,8},{8,10},{10,12},{12,14},{14,16},{16,18},{18... | collective-permute-start | bytes 245768 | tf_op jit(solution)/shard_map/ppermute | solution.py:419
  192.1 5.5 %collective-permute-start.32 = (bf16[144,128]{1,0:T(8,128)(2,1)S(1)}, bf16[144,128]{1,0:T(8,128)(2,1)S(1)}, u32[]{:S(2)}, u32[]{:S(2)}) collective-permute-start(bf16[144,128]{1,0:T(8,128)(2,1)S(1)} %get-tuple-element.139), channel_id=1, source_target_pairs={{0,64},{32,96},{64,0},{96,32},{1,65},{33,97},{65,1},{97,33},{2,66}... | collective-permute-start | bytes 110600 | tf_op jit(solution)/shard_map/ppermute | solution.py:125
  198.8 5.5 %collective-permute-start.35 = (bf16[144,128]{1,0:T(8,128)(2,1)S(1)}, bf16[144,128]{1,0:T(8,128)(2,1)S(1)}, u32[]{:S(2)}, u32[]{:S(2)}) collective-permute-start(bf16[144,128]{1,0:T(8,128)(2,1)S(1)} %shard_map.139.a), channel_id=1, source_target_pairs={{0,16},{8,24},{16,0},{24,8},{1,17},{9,25},{17,1},{25,9},{2,18},{10... | collective-permute-start | bytes 110600 | tf_op jit(solution)/shard_map/ppermute | solution.py:125
  205.6 5.7 %collective-permute-start.39 = (bf16[144,128]{1,0:T(8,128)(2,1)S(1)}, bf16[144,128]{1,0:T(8,128)(2,1)S(1)}, u32[]{:S(2)}, u32[]{:S(2)}) collective-permute-start(bf16[144,128]{1,0:T(8,128)(2,1)S(1)} %shard_map.140.p0), channel_id=1, source_target_pairs={{0,6},{2,0},{4,2},{6,4},{1,7},{3,1},{5,3},{7,5},{8,14},{10,8},{12,... | collective-permute-start | bytes 110600 | tf_op jit(solution)/shard_map/ppermute | solution.py:125
  209.6 5.6 %collective-permute-start.38 = (bf16[144,128]{1,0:T(8,128)(2,1)S(1)}, bf16[144,128]{1,0:T(8,128)(2,1)S(1)}, u32[]{:S(2)}, u32[]{:S(2)}) collective-permute-start(bf16[144,128]{1,0:T(8,128)(2,1)S(1)} %shard_map.140.p0), channel_id=1, source_target_pairs={{0,4},{2,6},{4,0},{6,2},{1,5},{3,7},{5,1},{7,3},{8,12},{10,14},{12... | collective-permute-start | bytes 110600 | tf_op jit(solution)/shard_map/ppermute | solution.py:125
  209.6 5.6 %collective-permute-start.37 = (bf16[144,128]{1,0:T(8,128)(2,1)S(1)}, bf16[144,128]{1,0:T(8,128)(2,1)S(1)}, u32[]{:S(2)}, u32[]{:S(2)}) collective-permute-start(bf16[144,128]{1,0:T(8,128)(2,1)S(1)} %shard_map.140.p0), channel_id=1, source_target_pairs={{0,2},{2,4},{4,6},{6,0},{1,3},{3,5},{5,7},{7,1},{8,10},{10,12},{12... | collective-permute-start | bytes 110600 | tf_op jit(solution)/shard_map/ppermute | solution.py:125
  220.1 5.5 %collective-permute-start.42 = (f32[16,640]{1,0:T(8,128)S(1)}, f32[16,640]{1,0:T(8,128)S(1)}, u32[]{:S(2)}, u32[]{:S(2)}) collective-permute-start(f32[16,640]{1,0:T(8,128)S(1)} %pad_maximum_fusion.1.a0), channel_id=1, source_target_pairs={{0,64},{32,96},{64,0},{96,32},{1,65},{33,97},{65,1},{97,33},{2,66}... | collective-permute-start | bytes 122888 | tf_op jit(solution)/shard_map/ppermute | solution.py:125
  228.4 16.8 %collective-permute-start.44 = (bf16[64,640]{1,0:T(8,128)(2,1)S(1)}, bf16[64,640]{1,0:T(8,128)(2,1)S(1)}, u32[]{:S(2)}, u32[]{:S(2)}) collective-permute-start(bf16[64,640]{1,0:T(8,128)(2,1)S(1)} %get-tuple-element.159), channel_id=1, source_target_pairs={{2,0},{4,2},{6,4},{8,6},{10,8},{12,10},{14,12},{16,14},{18,16},{20... | collective-permute-start | bytes 245768 | tf_op jit(solution)/shard_map/ppermute | solution.py:418
  229.9 15.2 %collective-permute-start.45 = (bf16[64,640]{1,0:T(8,128)(2,1)S(1)}, bf16[64,640]{1,0:T(8,128)(2,1)S(1)}, u32[]{:S(2)}, u32[]{:S(2)}) collective-permute-start(bf16[64,640]{1,0:T(8,128)(2,1)S(1)} %get-tuple-element.160), channel_id=1, source_target_pairs={{0,2},{2,4},{4,6},{6,8},{8,10},{10,12},{12,14},{14,16},{16,18},{18... | collective-permute-start | bytes 245768 | tf_op jit(solution)/shard_map/ppermute | solution.py:419
  (84 other events, 930.8 us)

commit v2 on v1

--- a/solution.py
+++ b/solution.py
@@ -36,9 +36,9 @@
     return jnp.concatenate([high, low], 0)
 
 
-def nt_wide(value, b):
+def nn_wide(value, b):
     rows = value.shape[0]
-    both = nt(two_parts(value), b)
+    both = nn(two_parts(value), b)
     return both[:rows] + both[rows:]
 
 
@@ -50,7 +50,7 @@
     return jnp.sum(value, keepdims=True)
 
 
-def call(kernel, outs, args, spaces, scratch=(), limit=16, flops=10**8):
+def call(kernel, outs, args, spaces, scratch=(), limit=6, flops=10**8):
     where = {"v": pltpu.VMEM, "m": pltpu.VMEM, "s": pltpu.SMEM}
     args = [
         pltpu.with_memory_space_constraint(a, pltpu.VMEM) if s == "m" else a
@@ -92,7 +92,7 @@
 def emit(me, sums, outs, num, den):
     share = sums[0].shape[0] // SIDE
     for k, out in enumerate(outs):
-        first = pl.multiple_of(lax.rem(me + k, SIDE) * share, share)
+        first = pl.multiple_of(jnp.bitwise_xor(me, k) * share, share)
         row = 0
         for chunk in range(sums[0].shape[1] // 128):
             for one in sums:
@@ -103,7 +103,7 @@
 
 def added(parts):
     p = [part[...].astype(F32) for part in parts]
-    return (p[0] + p[2]) + (p[1] + p[3])
+    return (p[0] + p[1]) + (p[2] + p[3])
 
 
 def sum_kernel(a, b, c, d, out):
@@ -122,7 +122,7 @@
 def swapped(values, axis):
     got = [values[0]]
     for k in range(1, SIDE):
-        got.append(lax.ppermute(values[k], axis, [(i, (i + k) % SIDE) for i in range(SIDE)]))
+        got.append(lax.ppermute(values[k], axis, [(i, i ^ k) for i in range(SIDE)]))
     return got
 
 
@@ -142,15 +142,72 @@
     return arrays, scalars_of(value[-tail:])
 
 
-def edge_start(counts, x, e, up, down):
+def load(d_in, e_in, c_in, inv_in, dt, et, e, ct, c, invt, stage, sems):
+    slots = e.shape[0]
+
+    def copies(m):
+        slot = lax.rem(m, 2)
+        return (
+            pltpu.make_async_copy(d_in.at[m], stage.at[0, slot], sems.at[0, slot]),
+            pltpu.make_async_copy(inv_in.at[m], stage.at[1, slot], sems.at[1, slot]),
+            pltpu.make_async_copy(e_in.at[m], e.at[m], sems.at[2, slot]),
+            pltpu.make_async_copy(c_in.at[m], c.at[m], sems.at[3, slot]),
+        )
+
+    for copy in copies(0):
+        copy.start()
+
+    @pl.loop(0, slots)
+    def _(m):
+        @pl.when(m + 1 < slots)
+        def _():
+            for copy in copies(m + 1):
+                copy.start()
+
+        for copy in copies(m):
+            copy.wait()
+        slot = lax.rem(m, 2)
+        dt[m] = stage[0, slot].T
+        invt[m] = stage[1, slot].T
+        et[m] = e[m].T
+        ct[m] = c[m].T
+
+
+def resident(diag, coupling, border_coupling, inverse):
+    slots, rows, border = border_coupling.shape
+    square, tall, flat = (slots, rows, rows), (slots, rows, border), (slots, border, rows)
+    shapes = (square, square, square, flat, tall, square)
+    return pl.pallas_call(
+        load,
+        out_shape=[pltpu.VMEM(shape, BF16) for shape in shapes],
+        in_specs=[pl.BlockSpec(memory_space=pltpu.HBM)] * 4,
+        out_specs=[pl.BlockSpec(memory_space=pltpu.VMEM)] * 6,
+        scratch_shapes=[pltpu.VMEM((2, 2, rows, rows), BF16), pltpu.SemaphoreType.DMA((4, 2))],
+        compiler_params=pltpu.CompilerParams(vmem_limit_bytes=8 * MIB),
+        cost_estimate=pl.CostEstimate(flops=10**9, bytes_accessed=25 * 10**6, transcendentals=0),
+    )(*(pltpu.with_memory_space_constraint(a, pltpu.HBM) for a in (diag, coupling, border_coupling, inverse)))
+
+
+def put_halo(odd, up, down, first, second):
+    odd = jnp.broadcast_to(odd, up.shape) == 1
+    first[...] = jnp.where(odd, up, down).astype(BF16)
+    second[...] = jnp.where(odd, down, up).astype(BF16)
+
+
+def from_halo(odd, first, second):
+    a, b = first[...].astype(F32), second[...].astype(F32)
+    odd = jnp.broadcast_to(odd, a.shape) == 1
+    return jnp.where(odd, b, a).astype(BF16), jnp.where(odd, a, b)
+
+
+def edge_start(counts, me, x, e, first, second):
     last = x.shape[0] - 1
     rows = x.shape[2]
-    up[...] = (x[0] * live_row(counts, 0, rows)).astype(BF16)
     tail = (x[last] * live_row(counts, last, rows)).astype(BF16)
-    down[...] = nn(tail, e[last]).astype(BF16)
-
-
-def inner_start(counts, x, b, border, d, e, c, inv, r, y, edge, t, g, v):
+    put_halo(me[1], x[0] * live_row(counts, 0, rows), nn(tail, e[0]), first, second)
+
+
+def inner_start(counts, x, b, border, dt, et, e, ct, c, invt, r, y, edge, t, g, v):
     slots, _, rows = x.shape
     for m in range(slots):
         v[m] = (x[m] * live_row(counts, m, rows)).astype(BF16)
@@ -161,9 +218,9 @@
     @pl.loop(1, slots - 1)
     def _(m):
         live = live_row(counts, m, rows)
-        q = nt(v[m], d[m]) + nt(v[m + 1], e[m]) + nn(v[m - 1], e[m - 1]) + nt(narrow, c[m])
+        q = nn(v[m], dt[m]) + nn(v[m + 1], et[m]) + nn(v[m - 1], e[m - 1]) + nn(narrow, ct[m])
         res = live * (b[m] - q)
-        blockwise = live * nt_wide(res, inv[m])
+        blockwise = live * nn_wide(res, invt[m])
         r[m - 1] = res
         y[m - 1] = blockwise
         both = nn(jnp.concatenate([blockwise.astype(BF16), v[m]], 0), c[m])
@@ -171,20 +228,21 @@
         g[...] += both[t.shape[0] :]
 
     z = slots - 1
-    edge[0] = nt(v[0], d[0]) + nt(v[1], e[0]) + nt(narrow, c[0])
-    edge[1] = nt(v[z], d[z]) + nn(v[z - 1], e[z - 1]) + nt(narrow, c[z])
-
-
-def outer_start(counts, me, x, b, edge, up, down, e, c, inv, t_in, g_in, r, y, s0, s1, s2, s3, t, g):
+    edge[0] = nn(v[0], dt[0]) + nn(v[1], et[0]) + nn(narrow, ct[0])
+    edge[1] = nn(v[z], dt[z]) + nn(v[z - 1], e[z - 1]) + nn(narrow, ct[z])
+
+
+def outer_start(counts, me, x, b, edge, first, second, et, c, invt, t_in, g_in, r, y, s0, s1, s2, s3, t, g):
     slots, _, rows = x.shape
     z = slots - 1
     t[...] = t_in[...]
     g[...] = g_in[...]
+    ahead, behind = from_halo(me[1], first, second)
     for i, m in enumerate((0, z)):
         live = live_row(counts, m, rows)
-        other = down[...].astype(F32) if i == 0 else nt(up[...], e[z])
+        other = behind if i == 0 else nn(ahead, et[z])
         res = live * (b[m] - (edge[i] + other))
-        blockwise = live * nt_wide(res, inv[m])
+        blockwise = live * nn_wide(res, invt[m])
         r[i] = res
         y[i] = blockwise
         v = (x[m] * live).astype(BF16)
@@ -236,36 +294,35 @@
     share = parts[0].shape[0]
     border = wb.shape[1]
     for k, part in enumerate(parts):
-        rows = pl.ds(pl.multiple_of(lax.rem(me + SIDE - k, SIDE) * share, share), share)
+        rows = pl.ds(pl.multiple_of(jnp.bitwise_xor(me, k) * share, share), share)
         if old is None:
             wb[rows, :] = part[:, :border]
         else:
             wb[rows, :] = old[rows, :] + scale * part[:, :border]
 
 
-def edge_update(counts, narrow, yv, c, inv, e, w, u, up, down, slots, rows):
+def edge_update(counts, odd, narrow, yv, ct, invt, e, w, u, first, second):
+    slots, rows, _ = invt.shape
     z = slots - 1
+    values = []
     for i, m in enumerate((0, z)):
-        live = live_row(counts, m, rows)
-        lift = nt(narrow, c[m])
+        lift = nn(narrow, ct[m])
         u[i] = lift
-        value = yv[i] - live * nt(lift.astype(BF16), inv[m])
+        value = yv[i] - live_row(counts, m, rows) * nn(lift.astype(BF16), invt[m])
         w[i] = value
-        if i == 0:
-            up[...] = value.astype(BF16)
-        else:
-            down[...] = nn(value.astype(BF16), e[z]).astype(BF16)
-
-
-def edge_first(counts, me, a0, a1, a2, a3, y, c, inv, e, wb, w, u, up, down):
+        values.append(value)
+    put_halo(odd, values[0], nn(values[1].astype(BF16), e[z]), first, second)
+
+
+def edge_first(counts, me, a0, a1, a2, a3, y, ct, invt, e, wb, w, u, first, second):
     place(me[0], (a0, a1, a2, a3), wb, None, None)
     yv = [y[0], y[1]]
-    edge_update(counts, wb[...].astype(BF16), yv, c, inv, e, w, u, up, down, inv.shape[0], inv.shape[1])
+    edge_update(counts, me[1], wb[...].astype(BF16), yv, ct, invt, e, w, u, first, second)
 
 
 def edge_next(
-    counts, me, a0, a1, a2, a3, wb_in, sol_in, rb_in, qb, y_in, p, r_in, q, c, inv, e,
-    alpha, wb, sol, rb, y, r, w, u, up, down,
+    counts, me, a0, a1, a2, a3, wb_in, sol_in, rb_in, qb, y_in, p, r_in, q, ct, invt, e,
+    alpha, wb, sol, rb, y, r, w, u, first, second,
 ):
     parts = (a0, a1, a2, a3)
     border = wb.shape[1]
@@ -281,11 +338,11 @@
         value = y_in[i] - a * p[i]
         y[i] = value
         yv.append(value)
-    edge_update(counts, wb[...].astype(BF16), yv, c, inv, e, w, u, up, down, inv.shape[0], inv.shape[1])
-
-
-def inner_body(counts, load, narrow, w_edge, u_edge, d, e, c, inv, w, q, p, edge, t, g, num, den, v, u, keep):
-    slots, rows, _ = inv.shape
+    edge_update(counts, me[1], wb[...].astype(BF16), yv, ct, invt, e, w, u, first, second)
+
+
+def inner_body(counts, load, narrow, w_edge, u_edge, dt, et, e, ct, c, invt, w, q, p, edge, t, g, num, den, v, u, keep):
+    slots, rows, _ = invt.shape
     z = slots - 1
     v[0] = w_edge[0].astype(BF16)
     v[z] = w_edge[1].astype(BF16)
@@ -293,9 +350,9 @@
     @pl.loop(1, z)
     def _(m):
         live = live_row(counts, m, rows)
-        lift = nt(narrow, c[m])
+        lift = nn(narrow, ct[m])
         u[m] = lift
-        value = load(m) - live * nt(lift.astype(BF16), inv[m])
+        value = load(m) - live * nn(lift.astype(BF16), invt[m])
         w[m - 1] = value
         v[m] = value.astype(BF16)
 
@@ -308,32 +365,32 @@
     @pl.loop(1, z)
     def _(m):
         live = live_row(counts, m, rows)
-        value = live * (nt(v[m], d[m]) + nt(v[m + 1], e[m]) + nn(v[m - 1], e[m - 1]) + u[m])
+        value = live * (nn(v[m], dt[m]) + nn(v[m + 1], et[m]) + nn(v[m - 1], e[m - 1]) + u[m])
         num[...] += jnp.sum(keep(m) * value, 0, keepdims=True)
         den[...] += jnp.sum(value * value, 0, keepdims=True)
         if t is None:
             g[...] += nn(v[m], c[m])
         else:
             q[m - 1] = value
-            back = live * nt_wide(value, inv[m])
+            back = live * nn_wide(value, invt[m])
             p[m - 1] = back
             both = nn(jnp.concatenate([back.astype(BF16), v[m]], 0), c[m])
             t[...] += both[: t.shape[0]]
             g[...] += both[t.shape[0] :]
 
-    edge[0] = nt(v[0], d[0]) + nt(v[1], e[0]) + u_edge[0]
-    edge[1] = nt(v[z], d[z]) + nn(v[z - 1], e[z - 1]) + u_edge[1]
-
-
-def inner_first(counts, wb, w_edge, u_edge, y, r, d, e, c, inv, w, q, p, edge, t, g, num, den, v, u):
+    edge[0] = nn(v[0], dt[0]) + nn(v[1], et[0]) + u_edge[0]
+    edge[1] = nn(v[z], dt[z]) + nn(v[z - 1], e[z - 1]) + u_edge[1]
+
+
+def inner_first(counts, wb, w_edge, u_edge, y, r, dt, et, e, ct, c, invt, w, q, p, edge, t, g, num, den, v, u):
     inner_body(
-        counts, lambda m: y[m - 1], wb[...].astype(BF16), w_edge, u_edge, d, e, c, inv,
+        counts, lambda m: y[m - 1], wb[...].astype(BF16), w_edge, u_edge, dt, et, e, ct, c, invt,
         w, q, p, edge, t, g, num, den, v, u, lambda m: r[m - 1],
     )
 
 
 def inner_next(
-    counts, alpha, wb, w_edge, u_edge, y_in, p_in, r_in, q_in, d, e, c, inv,
+    counts, alpha, wb, w_edge, u_edge, y_in, p_in, r_in, q_in, dt, et, e, ct, c, invt,
     y, r, w, q, p, edge, t, g, num, den, v, u,
 ):
     a = alpha[0:1, 0:1]
@@ -344,32 +401,33 @@
         return y[m - 1]
 
     inner_body(
-        counts, load, wb[...].astype(BF16), w_edge, u_edge, d, e, c, inv,
+        counts, load, wb[...].astype(BF16), w_edge, u_edge, dt, et, e, ct, c, invt,
         w, q, p, edge, t, g, num, den, v, u, lambda m: r[m - 1],
     )
 
 
 def inner_last(
-    counts, alpha, wb, w_edge, u_edge, y_in, p_in, r_in, q_in, d, e, c, inv,
+    counts, alpha, wb, w_edge, u_edge, y_in, p_in, r_in, q_in, dt, et, e, ct, c, invt,
     w, edge, g, num, den, v, u,
 ):
     a = alpha[0:1, 0:1]
     inner_body(
-        counts, lambda m: y_in[m - 1] - a * p_in[m - 1], wb[...].astype(BF16), w_edge, u_edge, d, e, c, inv,
+        counts, lambda m: y_in[m - 1] - a * p_in[m - 1], wb[...].astype(BF16), w_edge, u_edge, dt, et, e, ct, c, invt,
         w, None, None, edge, None, g, num, den, v, u, lambda m: r_in[m - 1] - a * q_in[m - 1],
     )
 
 
-def outer_body(counts, me, w_edge, r_edge, edge, up, down, e, c, inv, t_in, g_in, num_in, den_in, q, p, shares, t, g):
-    slots, rows, _ = inv.shape
+def outer_body(counts, me, w_edge, r_edge, edge, first, second, et, c, invt, t_in, g_in, num_in, den_in, q, p, shares, t, g):
+    slots, rows, _ = invt.shape
     z = slots - 1
+    ahead, behind = from_halo(me[1], first, second)
     if t is not None:
         t[...] = t_in[...]
     g[...] = g_in[...]
     num, den = total(num_in[...]), total(den_in[...])
     for i, m in enumerate((0, z)):
         live = live_row(counts, m, rows)
-        other = down[...].astype(F32) if i == 0 else nt(up[...], e[z])
+        other = behind if i == 0 else nn(ahead, et[z])
         value = live * (edge[i] + other)
         num += total(r_edge[i] * value)
         den += total(value * value)
@@ -378,7 +436,7 @@
             g[...] += nn(v, c[m])
         else:
             q[i] = value
-            back = live * nt_wide(value, inv[m])
+            back = live * nn_wide(value, invt[m])
             p[i] = back
             both = nn(jnp.concatenate([back.astype(BF16), v], 0), c[m])
             t[...] += both[: t.shape[0]]
@@ -386,15 +444,15 @@
     emit(me[0], (g,) if t is None else (t, g), shares, num, den)
 
 
-def outer_step(counts, me, w_edge, r_edge, edge, up, down, e, c, inv, t_in, g_in, num, den, q, p, s0, s1, s2, s3, t, g):
+def outer_step(counts, me, w_edge, r_edge, edge, first, second, et, c, invt, t_in, g_in, num, den, q, p, s0, s1, s2, s3, t, g):
     outer_body(
-        counts, me, w_edge, r_edge, edge, up, down, e, c, inv, t_in, g_in, num, den, q, p, (s0, s1, s2, s3), t, g
-    )
-
-
-def outer_last(counts, me, w_edge, r_edge, edge, up, down, e, c, inv, g_in, num, den, s0, s1, s2, s3, g):
+        counts, me, w_edge, r_edge, edge, first, second, et, c, invt, t_in, g_in, num, den, q, p, (s0, s1, s2, s3), t, g
+    )
+
+
+def outer_last(counts, me, w_edge, r_edge, edge, first, second, et, c, invt, g_in, num, den, s0, s1, s2, s3, g):
     outer_body(
-        counts, me, w_edge, r_edge, edge, up, down, e, c, inv, None, g_in, num, den, None, None,
+        counts, me, w_edge, r_edge, edge, first, second, et, c, invt, None, g_in, num, den, None, None,
         (s0, s1, s2, s3), None, g,
     )
 
@@ -413,11 +471,13 @@
         out[m] = ((x[m] * live_row(counts, m, rows) + c0 * a) + c1 * b) + step * c
 
 
-def halo(up, down):
+def halo(first, second):
     count = lax.axis_size(AXES)
-    ahead = lax.ppermute(up, AXES, [(i + 1, i) for i in range(count - 1)])
-    behind = lax.ppermute(down, AXES, [(i, i + 1) for i in range(count - 1)])
-    return ahead, behind
+    pairs = [(i, i ^ 1) for i in range(count)]
+    others = [(i, i + 1) for i in range(1, count - 1, 2)]
+    first = lax.ppermute(first, AXES, pairs)
+    second = lax.ppermute(second, AXES, others + [(j, i) for i, j in others])
+    return first, second
 
 
 def shards(
@@ -430,7 +490,7 @@
     slots, columns, rows = x.shape
     border = border_x.shape[1]
     share = columns // SIDE
-    me = lax.axis_index(AXES[0]).reshape(1).astype(jnp.int32)
+    me = jnp.stack([lax.axis_index(AXES[0]), lax.rem(lax.axis_index(AXES), 2)]).astype(jnp.int32)
     state, edges = ((slots - 2, columns, rows), F32), ((2, columns, rows), F32)
     one16, wide = ((columns, rows), BF16), ((columns, border), F32)
     line, piece = ((1, rows), F32), ((share, border), F32)
@@ -442,20 +502,22 @@
     def message(dtype, sums):
         return ((share * sums * border // 128 + tail_rows(dtype), 128), dtype)
 
-    up, down = call(edge_start, [one16, one16], [counts, x, coupling], "svm")
+    up, down = call(edge_start, [one16, one16], [counts, me, x, coupling[slots - 1 :]], "ssvv")
     up, down = halo(up, down)
+    matrices = resident(diag, coupling, border_coupling, inverse)
+    dt, et, e, ct, c, invt = matrices
     r, y, edge, t, g = call(
         inner_start,
         [state, state, edges, wide, wide],
-        [counts, x, b, border_x, diag, coupling, border_coupling, inverse],
-        "svvvmmmm",
+        [counts, x, b, border_x, *matrices],
+        "svvvmmmmmm",
         [keep16],
         flops=4 * 10**9,
     )
     r_edge, y_edge, *shares = call(
         outer_start,
         [edges, edges] + [message(WIRE[0], 2)] * SIDE,
-        [counts, me, x, b, edge, up, down, coupling, border_coupling, inverse, t, g],
+        [counts, me, x, b, edge, up, down, et, c, invt, t, g],
         "ssvvvvvmmmvv",
         [acc, acc],
         flops=5 * 10**8,
@@ -475,7 +537,7 @@
             wb, w_edge, u_edge, up, down = call(
                 edge_first,
                 [wide, edges, edges, one16, one16],
-                [counts, me, *gathered, y_edge, border_coupling, inverse, coupling],
+                [counts, me, *gathered, y_edge, ct, invt, e],
                 "ssvvvvvmmm",
                 flops=5 * 10**8,
             )
@@ -484,19 +546,18 @@
                 edge_next,
                 [tile, wide, wide, piece, edges, edges, edges, edges, one16, one16],
                 [counts, me, *gathered, wb, sol, rb, qb, y_edge, p_edge, r_edge, q_edge]
-                + [border_coupling, inverse, coupling],
+                + [ct, invt, e],
                 "ss" + "v" * 12 + "mmm",
                 flops=5 * 10**8,
             )
             steps.append(step)
         up, down = halo(up, down)
-        matrices = [diag, coupling, border_coupling, inverse]
         if k == 0:
             w, q, p, edge, t, g, num, den = call(
                 inner_first,
                 [state, state, state, edges, wide, wide, line, line],
-                [counts, wb, w_edge, u_edge, y, r] + matrices,
-                "svvvvvmmmm",
+                [counts, wb, w_edge, u_edge, y, r, *matrices],
+                "svvvvvmmmmmm",
                 [keep16, keep32],
                 flops=4 * 10**9,
             )
@@ -504,24 +565,23 @@
             y, r, w, q, p, edge, t, g, num, den = call(
                 inner_next,
                 [state, state, state, state, state, edges, wide, wide, line, line],
-                [counts, step, wb, w_edge, u_edge, y, p, r, q] + matrices,
-                "s" + "v" * 8 + "mmmm",
+                [counts, step, wb, w_edge, u_edge, y, p, r, q, *matrices],
+                "s" + "v" * 8 + "mmmmmm",
                 [keep16, keep32],
-                limit=24,
                 flops=4 * 10**9,
             )
         else:
             w, edge, g, num, den = call(
                 inner_last,
                 [state, edges, wide, line, line],
-                [counts, step, wb, w_edge, u_edge, y, p, r, q] + matrices,
-                "s" + "v" * 8 + "mmmm",
+                [counts, step, wb, w_edge, u_edge, y, p, r, q, *matrices],
+                "s" + "v" * 8 + "mmmmmm",
                 [keep16, keep32],
                 flops=3 * 10**9,
             )
         edge_updates.append(w_edge)
         updates.append(w)
-        inputs = [counts, me, w_edge, r_edge, edge, up, down, coupling, border_coupling, inverse]
+        inputs = [counts, me, w_edge, r_edge, edge, up, down, et, c, invt]
         if not last:
             q_edge, p_edge, *shares = call(
                 outer_step,
@@ -565,7 +625,6 @@
         [(x.shape, F32), wide],
         [counts, *gathered, wb, sol, x, *steps, *edge_updates, *updates],
         "s" + "v" * 15,
-        limit=24,
     )
     return out.transpose(0, 2, 1), border_out.T
 

time: 283 us -> 223 us (0.79)
  local copies, waits for them, and re-layouts: 43.8 us -> 3.25 us
  waiting for transfers between devices: 68.8 us -> 56.8 us
  starting transfers between devices: 96.8 us -> 93.2 us
    unnamed x114 -> x32, local copies, waits for them, and re-layouts: 43.8 us -> 2.03 us
    pallas_call x28, Pallas kernels: 71.4 us -> 56.3 us  [call(): pl.pallas_call(kernel, out_shape=[jax.ShapeDtypeStruct(*o) for o in outs]...]
    pallas_call x0 -> x1, Pallas kernels: none -> 12.4 us  [resident(): pl.pallas_call(load, out_shape=[pltpu.VMEM(shape, BF16) for shape in shap...]
    ppermute x56, waiting for transfers between devices: 67.2 us -> 55.2 us  [the longest x48 55.1 us: swapped(): got.append(lax.ppermute(values[k], axis, [(i, i ^ k) for i in range(SIDE)]))]
    ppermute x56, starting transfers between devices: 96.4 us -> 93 us  [the longest x48 84.8 us: swapped(): got.append(lax.ppermute(values[k], axis, [(i, i ^ k) for i in range(SIDE)]))]
  transfers between devices with their start and end apart: 59 -> 59, of which waited for: 47 -> 41; matrix products, arithmetic and copies ran while one was open for 0% -> 0% of each run, Pallas kernels for 18% -> 22%
where the time goes in v2:
time: 223 us
  starting transfers between devices  93.2 us (42%)
  Pallas kernels  68.6 us (31%)
  waiting for transfers between devices  56.8 us (25%)
  local copies, waits for them, and re-layouts  3.25 us (1%)
    ppermute x48, starting transfers between devices, swapped(): got.append(lax.ppermute(values[k], axis, [(i, i ^ k) for i in range(SIDE)]))  84.8 us
    pallas_call x28, Pallas kernels, call(): pl.pallas_call(kernel, out_shape=[jax.ShapeDtypeStruct(*o) for o in outs]...  56.3 us
    ppermute x48, waiting for transfers between devices, swapped(): got.append(lax.ppermute(values[k], axis, [(i, i ^ k) for i in range(SIDE)]))  55.1 us
    pallas_call x1, Pallas kernels, resident(): pl.pallas_call(load, out_shape=[pltpu.VMEM(shape, BF16) for shape in shap...  12.4 us
    ppermute x4, starting transfers between devices, halo(): first = lax.ppermute(first, AXES, pairs)  5.19 us
  transfers between devices with their start and end apart: 59, of which 41 were waited for; matrix products, arithmetic and copies ran while one was open for 0% of the time, Pallas kernels for 22%

profile of v2, /device:TPU:0, one launch (start us, length us, event | category | flops | bytes accessed | tf_op | source)
XLA Modules:
  0.0 223.0 jit_solution(11661046593474402981)
XLA Ops:
  7.7 12.4 %shard_map.122 = (bf16[8,640,640]{2,1,0:T(8,128)(2,1)S(1)}, bf16[8,640,640]{2,1,0:T(8,128)(2,1)S(1)}, bf16[8,640,640]{2,1,0:T(8,128)(2,1)S(1)}, bf16[8,512,640]{...) custom-call(bf16[8,640,640]{2,1,0:T(8,128)(2,1)} %d_in.1, ...), custom_call_target="tpu_custom_call" | custom-call | flops 1000000000 | bytes 25000000 | tf_op jit(solution)/shard_map/pallas_call | solution.py:180
  20.1 7.9 %shard_map.123 = (f32[6,64,640]{2,1,0:T(8,128)S(1)}, f32[6,64,640]{2,1,0:T(8,128)S(1)}, f32[2,64,640]{2,1,0:T(8,128)S(1)}, f32[64,512]{1,0:T(8,128)S(1)}, f32[64,512]{1,0:T(8,128)S(1)}) custom-call(s32[8]{0:T(128)S(1)} %copy-done.9, f32[8,64,640]{2,1,0:T(8,128)S(1)} %bitcast.15, f32[8,64,640]{2,1,0:T(8,128)S(1)} %bitcast.18, f32[64,512]{1,0:T(8,128)S(1)} %bitcast.20, ...), custom_call_target="tpu_custom_call" | custom-call | flops 4000000000 | bytes 1000000 | tf_op jit(solution)/shard_map/pallas_call | solution.py:59
  29.6 7.9 %collective-permute-start.2 = (f32[136,128]{1,0:T(8,128)S(1)}, f32[136,128]{1,0:T(8,128)S(1)}, u32[]{:S(2)}, u32[]{:S(2)}) collective-permute-start(f32[136,128]{1,0:T(8,128)S(1)} %get-tuple-element.107), channel_id=1, source_target_pairs={{0,32},{32,0},{64,96},{96,64},{1,33},{33,1},{65,97},{97,65},{2,34}... | collective-permute-start | bytes 208904 | tf_op jit(solution)/shard_map/ppermute | solution.py:125
  37.5 3.0 %collective-permute-start.3 = (f32[136,128]{1,0:T(8,128)S(1)}, f32[136,128]{1,0:T(8,128)S(1)}, u32[]{:S(2)}, u32[]{:S(2)}) collective-permute-start(f32[136,128]{1,0:T(8,128)S(1)} %get-tuple-element.108), channel_id=1, source_target_pairs={{0,64},{32,96},{64,0},{96,32},{1,65},{33,97},{65,1},{97,33},{2,66}... | collective-permute-start | bytes 208904 | tf_op jit(solution)/shard_map/ppermute | solution.py:125
  40.5 3.1 %collective-permute-done.3.c = f32[136,128]{1,0:T(8,128)S(1)} collective-permute-done((f32[136,128]{1,0:T(8,128)S(1)}, f32[136,128]{1,0:T(8,128)S(1)}, u32[]{:S(2)}, u32[]{:S(2)}) %collective-permute-start.3) | collective-permute-done | bytes 69664 | tf_op jit(solution)/shard_map/ppermute | solution.py:125
  43.6 2.4 %collective-permute-done.4.d = f32[136,128]{1,0:T(8,128)S(1)} collective-permute-done((f32[136,128]{1,0:T(8,128)S(1)}, f32[136,128]{1,0:T(8,128)S(1)}, u32[]{:S(2)}, u32[]{:S(2)}) %collective-permute-start.4) | collective-permute-done | bytes 69664 | tf_op jit(solution)/shard_map/ppermute | solution.py:125
  47.0 3.3 %collective-permute-start.5 = (f32[136,128]{1,0:T(8,128)S(1)}, f32[136,128]{1,0:T(8,128)S(1)}, u32[]{:S(2)}, u32[]{:S(2)}) collective-permute-start(f32[136,128]{1,0:T(8,128)S(1)} %shard_map.126.a), channel_id=1, source_target_pairs={{0,8},{8,0},{16,24},{24,16},{1,9},{9,1},{17,25},{25,17},{2,10},{10... | collective-permute-start | bytes 208904 | tf_op jit(solution)/shard_map/ppermute | solution.py:125
  57.5 2.2 collective-permute-done.10.p3
  63.1 3.3 %collective-permute-start.11 = (f32[16,512]{1,0:T(8,128)S(1)}, f32[16,512]{1,0:T(8,128)S(1)}, u32[]{:S(2)}, u32[]{:S(2)}) collective-permute-start(f32[16,512]{1,0:T(8,128)S(1)} %shard_map.129.a0), channel_id=1, source_target_pairs={{0,32},{32,0},{64,96},{96,64},{1,33},{33,1},{65,97},{97,65},{2,34}... | collective-permute-start | bytes 98312 | tf_op jit(solution)/shard_map/ppermute | solution.py:125
  72.1 9.7 %shard_map.131 = (f32[6,64,640]{2,1,0:T(8,128)S(1)}, f32[6,64,640]{2,1,0:T(8,128)S(1)}, f32[6,64,640]{2,1,0:T(8,128)S(1)}, f32[2,64,640]{2,1,0:T(8,128)S(1)}, f3...) custom-call(s32[8]{0:T(128)S(1)} %copy-done.9, ...), custom_call_target="tpu_custom_call" | custom-call | flops 4000000000 | bytes 1000000 | tf_op jit(solution)/shard_map/pallas_call | solution.py:59
  83.5 4.8 %collective-permute-start.16 = (f32[136,128]{1,0:T(8,128)S(1)}, f32[136,128]{1,0:T(8,128)S(1)}, u32[]{:S(2)}, u32[]{:S(2)}) collective-permute-start(f32[136,128]{1,0:T(8,128)S(1)} %get-tuple-element.126), channel_id=1, source_target_pairs={{0,32},{32,0},{64,96},{96,64},{1,33},{33,1},{65,97},{97,65},{2,34}... | collective-permute-start | bytes 208904 | tf_op jit(solution)/shard_map/ppermute | solution.py:125
  91.1 3.0 %collective-permute-done.17.c = f32[136,128]{1,0:T(8,128)S(1)} collective-permute-done((f32[136,128]{1,0:T(8,128)S(1)}, f32[136,128]{1,0:T(8,128)S(1)}, u32[]{:S(2)}, u32[]{:S(2)}) %collective-permute-start.17) | collective-permute-done | bytes 69664 | tf_op jit(solution)/shard_map/ppermute | solution.py:125
  96.5 2.1 collective-permute-start.20
  103.1 2.7 %collective-permute-start.24 = (f32[136,128]{1,0:T(8,128)S(1)}, f32[136,128]{1,0:T(8,128)S(1)}, u32[]{:S(2)}, u32[]{:S(2)}) collective-permute-start(f32[136,128]{1,0:T(8,128)S(1)} %shard_map.134.p0), channel_id=1, source_target_pairs={{0,6},{2,4},{4,2},{6,0},{1,7},{3,5},{5,3},{7,1},{8,14},{10,12},{12... | collective-permute-start | bytes 208904 | tf_op jit(solution)/shard_map/ppermute | solution.py:125
  108.7 2.9 %collective-permute-done.23.p2 = f32[136,128]{1,0:T(8,128)S(1)} collective-permute-done((f32[136,128]{1,0:T(8,128)S(1)}, f32[136,128]{1,0:T(8,128)S(1)}, u32[]{:S(2)}, u32[]{:S(2)}) %collective-permute-start.23) | collective-permute-done | bytes 69664 | tf_op jit(solution)/shard_map/ppermute | solution.py:125
  113.8 2.6 %collective-permute-start.28 = (f32[16,640]{1,0:T(8,128)S(1)}, f32[16,640]{1,0:T(8,128)S(1)}, u32[]{:S(2)}, u32[]{:S(2)}) collective-permute-start(f32[16,640]{1,0:T(8,128)S(1)} %pad_maximum_fusion.a0), channel_id=1, source_target_pairs={{0,96},{32,64},{64,32},{96,0},{1,97},{33,65},{65,33},{97,1},{2,98}... | collective-permute-start | bytes 122888 | tf_op jit(solution)/shard_map/ppermute | solution.py:125
  119.1 2.8 %collective-permute-done.27.a2 = f32[16,640]{1,0:T(8,128)S(1)} collective-permute-done((f32[16,640]{1,0:T(8,128)S(1)}, f32[16,640]{1,0:T(8,128)S(1)}, u32[]{:S(2)}, u32[]{:S(2)}) %collective-permute-start.27) | collective-permute-done | bytes 40992 | tf_op jit(solution)/shard_map/ppermute | solution.py:125
  124.3 9.8 %shard_map.138 = (f32[6,64,640]{2,1,0:T(8,128)S(1)}, f32[6,64,640]{2,1,0:T(8,128)S(1)}, f32[6,64,640]{2,1,0:T(8,128)S(1)}, f32[6,64,640]{2,1,0:T(8,128)S(1)}, f3...) custom-call(s32[8]{0:T(128)S(1)} %copy-done.9, ...), custom_call_target="tpu_custom_call" | custom-call | flops 4000000000 | bytes 1000000 | tf_op jit(solution)/shard_map/pallas_call | solution.py:59
  135.8 6.1 %collective-permute-start.31 = (bf16[144,128]{1,0:T(8,128)(2,1)S(1)}, bf16[144,128]{1,0:T(8,128)(2,1)S(1)}, u32[]{:S(2)}, u32[]{:S(2)}) collective-permute-start(bf16[144,128]{1,0:T(8,128)(2,1)S(1)} %get-tuple-element.150), channel_id=1, source_target_pairs={{0,32},{32,0},{64,96},{96,64},{1,33},{33,1},{65,97},{97,65},{2,34}... | collective-permute-start | bytes 110600 | tf_op jit(solution)/shard_map/ppermute | solution.py:125
  144.6 2.7 %collective-permute-done.32.c = bf16[144,128]{1,0:T(8,128)(2,1)S(1)} collective-permute-done((bf16[144,128]{1,0:T(8,128)(2,1)S(1)}, bf16[144,128]{1,0:T(8,128)(2,1)S(1)}, u32[]{:S(2)}, u32[]{:S(2)}) %collective-permute-start.32) | collective-permute-done | bytes 36896 | tf_op jit(solution)/shard_map/ppermute | solution.py:125
  151.0 2.3 %collective-permute-start.34 = (bf16[144,128]{1,0:T(8,128)(2,1)S(1)}, bf16[144,128]{1,0:T(8,128)(2,1)S(1)}, u32[]{:S(2)}, u32[]{:S(2)}) collective-permute-start(bf16[144,128]{1,0:T(8,128)(2,1)S(1)} %shard_map.140.a), channel_id=1, source_target_pairs={{0,8},{8,0},{16,24},{24,16},{1,9},{9,1},{17,25},{25,17},{2,10},{10... | collective-permute-start | bytes 110600 | tf_op jit(solution)/shard_map/ppermute | solution.py:125
  156.7 3.1 %collective-permute-start.37 = (bf16[144,128]{1,0:T(8,128)(2,1)S(1)}, bf16[144,128]{1,0:T(8,128)(2,1)S(1)}, u32[]{:S(2)}, u32[]{:S(2)}) collective-permute-start(bf16[144,128]{1,0:T(8,128)(2,1)S(1)} %shard_map.141.p0), channel_id=1, source_target_pairs={{0,2},{2,0},{4,6},{6,4},{1,3},{3,1},{5,7},{7,5},{8,10},{10,8},{12,... | collective-permute-start | bytes 110600 | tf_op jit(solution)/shard_map/ppermute | solution.py:125
  166.0 2.6 %collective-permute-start.41 = (f32[16,640]{1,0:T(8,128)S(1)}, f32[16,640]{1,0:T(8,128)S(1)}, u32[]{:S(2)}, u32[]{:S(2)}) collective-permute-start(f32[16,640]{1,0:T(8,128)S(1)} %pad_maximum_fusion.1.a0), channel_id=1, source_target_pairs={{0,32},{32,0},{64,96},{96,64},{1,33},{33,1},{65,97},{97,65},{2,34}... | collective-permute-start | bytes 122888 | tf_op jit(solution)/shard_map/ppermute | solution.py:125
  171.5 2.2 shard_map.144
  176.2 7.6 %shard_map.145 = (f32[6,64,640]{2,1,0:T(8,128)S(1)}, f32[2,64,640]{2,1,0:T(8,128)S(1)}, f32[64,512]{1,0:T(8,128)S(1)}, f32[1,640]{1,0:T(1,128)S(1)}, f32[1,640]{1,0:T(1,128)S(1)}) custom-call(s32[8]{0:T(128)S(1)} %copy-done.9, f32[8,128]{1,0:T(8,128)S(1)} %get-tuple-element.163.alpha.al1, f32[64,512]{1,0:T(8,128)S(1)} %get-tuple-element.164.wb, ...), custom_call_target="tpu_custom_call" | custom-call | flops 3000000000 | bytes 1000000 | tf_op jit(solution)/shard_map/pallas_call | solution.py:59
  184.9 4.6 %collective-permute-start.46 = (bf16[80,128]{1,0:T(8,128)(2,1)S(1)}, bf16[80,128]{1,0:T(8,128)(2,1)S(1)}, u32[]{:S(2)}, u32[]{:S(2)}) collective-permute-start(bf16[80,128]{1,0:T(8,128)(2,1)S(1)} %get-tuple-element.177), channel_id=1, source_target_pairs={{0,32},{32,0},{64,96},{96,64},{1,33},{33,1},{65,97},{97,65},{2,34}... | collective-permute-start | bytes 61448 | tf_op jit(solution)/shard_map/ppermute | solution.py:125
  192.3 2.5 %collective-permute-done.47.c = bf16[80,128]{1,0:T(8,128)(2,1)S(1)} collective-permute-done((bf16[80,128]{1,0:T(8,128)(2,1)S(1)}, bf16[80,128]{1,0:T(8,128)(2,1)S(1)}, u32[]{:S(2)}, u32[]{:S(2)}) %collective-permute-start.47) | collective-permute-done | bytes 20512 | tf_op jit(solution)/shard_map/ppermute | solution.py:125
  202.5 2.8 %collective-permute-start.54 = (bf16[80,128]{1,0:T(8,128)(2,1)S(1)}, bf16[80,128]{1,0:T(8,128)(2,1)S(1)}, u32[]{:S(2)}, u32[]{:S(2)}) collective-permute-start(bf16[80,128]{1,0:T(8,128)(2,1)S(1)} %shard_map.148.p0), channel_id=1, source_target_pairs={{0,6},{2,4},{4,2},{6,0},{1,7},{3,5},{5,3},{7,1},{8,14},{10,12},{12... | collective-permute-start | bytes 61448 | tf_op jit(solution)/shard_map/ppermute | solution.py:125
  207.6 3.1 %collective-permute-done.53.p2 = bf16[80,128]{1,0:T(8,128)(2,1)S(1)} collective-permute-done((bf16[80,128]{1,0:T(8,128)(2,1)S(1)}, bf16[80,128]{1,0:T(8,128)(2,1)S(1)}, u32[]{:S(2)}, u32[]{:S(2)}) %collective-permute-start.53) | collective-permute-done | bytes 20512 | tf_op jit(solution)/shard_map/ppermute | solution.py:125
  213.2 2.5 %collective-permute-start.58 = (f32[16,128]{1,0:T(8,128)S(1)}, f32[16,128]{1,0:T(8,128)S(1)}, u32[]{:S(2)}, u32[]{:S(2)}) collective-permute-start(f32[16,128]{1,0:T(8,128)S(1)} %add.19.a0), channel_id=1, source_target_pairs={{0,96},{32,64},{64,32},{96,0},{1,97},{33,65},{65,33},{97,1},{2,98}... | collective-permute-start | bytes 24584 | tf_op jit(solution)/shard_map/ppermute | solution.py:125
  218.1 2.8 %collective-permute-done.57.a2 = f32[16,128]{1,0:T(8,128)S(1)} collective-permute-done((f32[16,128]{1,0:T(8,128)S(1)}, f32[16,128]{1,0:T(8,128)S(1)}, u32[]{:S(2)}, u32[]{:S(2)}) %collective-permute-start.57) | collective-permute-done | bytes 8224 | tf_op jit(solution)/shard_map/ppermute | solution.py:125
  220.9 2.2 shard_map.150
  (157 shorter events, 89.1 us)
Async XLA Ops:
  4.7 23.2 %collective-permute-start = (bf16[64,640]{1,0:T(8,128)(2,1)S(1)}, bf16[64,640]{1,0:T(8,128)(2,1)S(1)}, u32[]{:S(2)}, u32[]{:S(2)}) collective-permute-start(bf16[64,640]{1,0:T(8,128)(2,1)S(1)} %get-tuple-element.102), channel_id=1, source_target_pairs={{0,2},{2,0},{4,6},{6,4},{8,10},{10,8},{12,14},{14,12},{16,18},{18,... | collective-permute-start | bytes 245768 | tf_op jit(solution)/shard_map/ppermute | solution.py:478
  6.9 21.1 %collective-permute-start.1 = (bf16[64,640]{1,0:T(8,128)(2,1)S(1)}, bf16[64,640]{1,0:T(8,128)(2,1)S(1)}, u32[]{:S(2)}, u32[]{:S(2)}) collective-permute-start(bf16[64,640]{1,0:T(8,128)(2,1)S(1)} %get-tuple-element.103), channel_id=1, source_target_pairs={{2,4},{6,8},{10,12},{14,16},{18,20},{22,24},{26,28},{30,32},{34,36... | collective-permute-start | bytes 245768 | tf_op jit(solution)/shard_map/ppermute | solution.py:479
  29.6 10.9 %collective-permute-start.2 = (f32[136,128]{1,0:T(8,128)S(1)}, f32[136,128]{1,0:T(8,128)S(1)}, u32[]{:S(2)}, u32[]{:S(2)}) collective-permute-start(f32[136,128]{1,0:T(8,128)S(1)} %get-tuple-element.107), channel_id=1, source_target_pairs={{0,32},{32,0},{64,96},{96,64},{1,33},{33,1},{65,97},{97,65},{2,34}... | collective-permute-start | bytes 208904 | tf_op jit(solution)/shard_map/ppermute | solution.py:125
  37.5 6.1 %collective-permute-start.3 = (f32[136,128]{1,0:T(8,128)S(1)}, f32[136,128]{1,0:T(8,128)S(1)}, u32[]{:S(2)}, u32[]{:S(2)}) collective-permute-start(f32[136,128]{1,0:T(8,128)S(1)} %get-tuple-element.108), channel_id=1, source_target_pairs={{0,64},{32,96},{64,0},{96,32},{1,65},{33,97},{65,1},{97,33},{2,66}... | collective-permute-start | bytes 208904 | tf_op jit(solution)/shard_map/ppermute | solution.py:125
  40.5 5.5 %collective-permute-start.4 = (f32[136,128]{1,0:T(8,128)S(1)}, f32[136,128]{1,0:T(8,128)S(1)}, u32[]{:S(2)}, u32[]{:S(2)}) collective-permute-start(f32[136,128]{1,0:T(8,128)S(1)} %get-tuple-element.109), channel_id=1, source_target_pairs={{0,96},{32,64},{64,32},{96,0},{1,97},{33,65},{65,33},{97,1},{2,98}... | collective-permute-start | bytes 208904 | tf_op jit(solution)/shard_map/ppermute | solution.py:125
  46.1 5.6 %collective-permute-start.7 = (f32[136,128]{1,0:T(8,128)S(1)}, f32[136,128]{1,0:T(8,128)S(1)}, u32[]{:S(2)}, u32[]{:S(2)}) collective-permute-start(f32[136,128]{1,0:T(8,128)S(1)} %shard_map.126.a), channel_id=1, source_target_pairs={{0,24},{8,16},{16,8},{24,0},{1,25},{9,17},{17,9},{25,1},{2,26},{10... | collective-permute-start | bytes 208904 | tf_op jit(solution)/shard_map/ppermute | solution.py:125
  46.6 5.8 %collective-permute-start.6 = (f32[136,128]{1,0:T(8,128)S(1)}, f32[136,128]{1,0:T(8,128)S(1)}, u32[]{:S(2)}, u32[]{:S(2)}) collective-permute-start(f32[136,128]{1,0:T(8,128)S(1)} %shard_map.126.a), channel_id=1, source_target_pairs={{0,16},{8,24},{16,0},{24,8},{1,17},{9,25},{17,1},{25,9},{2,18},{10... | collective-permute-start | bytes 208904 | tf_op jit(solution)/shard_map/ppermute | solution.py:125
  47.0 6.3 %collective-permute-start.5 = (f32[136,128]{1,0:T(8,128)S(1)}, f32[136,128]{1,0:T(8,128)S(1)}, u32[]{:S(2)}, u32[]{:S(2)}) collective-permute-start(f32[136,128]{1,0:T(8,128)S(1)} %shard_map.126.a), channel_id=1, source_target_pairs={{0,8},{8,0},{16,24},{24,16},{1,9},{9,1},{17,25},{25,17},{2,10},{10... | collective-permute-start | bytes 208904 | tf_op jit(solution)/shard_map/ppermute | solution.py:125
  53.3 6.3 %collective-permute-start.10 = (f32[136,128]{1,0:T(8,128)S(1)}, f32[136,128]{1,0:T(8,128)S(1)}, u32[]{:S(2)}, u32[]{:S(2)}) collective-permute-start(f32[136,128]{1,0:T(8,128)S(1)} %shard_map.127.p0), channel_id=1, source_target_pairs={{0,6},{2,4},{4,2},{6,0},{1,7},{3,5},{5,3},{7,1},{8,14},{10,12},{12... | collective-permute-start | bytes 208904 | tf_op jit(solution)/shard_map/ppermute | solution.py:125
  53.4 6.3 %collective-permute-start.9 = (f32[136,128]{1,0:T(8,128)S(1)}, f32[136,128]{1,0:T(8,128)S(1)}, u32[]{:S(2)}, u32[]{:S(2)}) collective-permute-start(f32[136,128]{1,0:T(8,128)S(1)} %shard_map.127.p0), channel_id=1, source_target_pairs={{0,4},{2,6},{4,0},{6,2},{1,5},{3,7},{5,1},{7,3},{8,12},{10,14},{12... | collective-permute-start | bytes 208904 | tf_op jit(solution)/shard_map/ppermute | solution.py:125
  63.1 5.5 %collective-permute-start.11 = (f32[16,512]{1,0:T(8,128)S(1)}, f32[16,512]{1,0:T(8,128)S(1)}, u32[]{:S(2)}, u32[]{:S(2)}) collective-permute-start(f32[16,512]{1,0:T(8,128)S(1)} %shard_map.129.a0), channel_id=1, source_target_pairs={{0,32},{32,0},{64,96},{96,64},{1,33},{33,1},{65,97},{97,65},{2,34}... | collective-permute-start | bytes 98312 | tf_op jit(solution)/shard_map/ppermute | solution.py:125
  70.1 11.8 %collective-permute-start.14 = (bf16[64,640]{1,0:T(8,128)(2,1)S(1)}, bf16[64,640]{1,0:T(8,128)(2,1)S(1)}, u32[]{:S(2)}, u32[]{:S(2)}) collective-permute-start(bf16[64,640]{1,0:T(8,128)(2,1)S(1)} %get-tuple-element.119), channel_id=1, source_target_pairs={{0,2},{2,0},{4,6},{6,4},{8,10},{10,8},{12,14},{14,12},{16,18},{18,... | collective-permute-start | bytes 245768 | tf_op jit(solution)/shard_map/ppermute | solution.py:478
  71.4 10.4 %collective-permute-start.15 = (bf16[64,640]{1,0:T(8,128)(2,1)S(1)}, bf16[64,640]{1,0:T(8,128)(2,1)S(1)}, u32[]{:S(2)}, u32[]{:S(2)}) collective-permute-start(bf16[64,640]{1,0:T(8,128)(2,1)S(1)} %get-tuple-element.120), channel_id=1, source_target_pairs={{2,4},{6,8},{10,12},{14,16},{18,20},{22,24},{26,28},{30,32},{34,36... | collective-permute-start | bytes 245768 | tf_op jit(solution)/shard_map/ppermute | solution.py:479
  83.5 7.6 %collective-permute-start.16 = (f32[136,128]{1,0:T(8,128)S(1)}, f32[136,128]{1,0:T(8,128)S(1)}, u32[]{:S(2)}, u32[]{:S(2)}) collective-permute-start(f32[136,128]{1,0:T(8,128)S(1)} %get-tuple-element.126), channel_id=1, source_target_pairs={{0,32},{32,0},{64,96},{96,64},{1,33},{33,1},{65,97},{97,65},{2,34}... | collective-permute-start | bytes 208904 | tf_op jit(solution)/shard_map/ppermute | solution.py:125
  88.3 5.8 %collective-permute-start.17 = (f32[136,128]{1,0:T(8,128)S(1)}, f32[136,128]{1,0:T(8,128)S(1)}, u32[]{:S(2)}, u32[]{:S(2)}) collective-permute-start(f32[136,128]{1,0:T(8,128)S(1)} %get-tuple-element.127), channel_id=1, source_target_pairs={{0,64},{32,96},{64,0},{96,32},{1,65},{33,97},{65,1},{97,33},{2,66}... | collective-permute-start | bytes 208904 | tf_op jit(solution)/shard_map/ppermute | solution.py:125
  90.2 5.5 %collective-permute-start.18 = (f32[136,128]{1,0:T(8,128)S(1)}, f32[136,128]{1,0:T(8,128)S(1)}, u32[]{:S(2)}, u32[]{:S(2)}) collective-permute-start(f32[136,128]{1,0:T(8,128)S(1)} %get-tuple-element.128), channel_id=1, source_target_pairs={{0,96},{32,64},{64,32},{96,0},{1,97},{33,65},{65,33},{97,1},{2,98}... | collective-permute-start | bytes 208904 | tf_op jit(solution)/shard_map/ppermute | solution.py:125
  95.7 5.8 %collective-permute-start.21 = (f32[136,128]{1,0:T(8,128)S(1)}, f32[136,128]{1,0:T(8,128)S(1)}, u32[]{:S(2)}, u32[]{:S(2)}) collective-permute-start(f32[136,128]{1,0:T(8,128)S(1)} %shard_map.133.a), channel_id=1, source_target_pairs={{0,24},{8,16},{16,8},{24,0},{1,25},{9,17},{17,9},{25,1},{2,26},{10... | collective-permute-start | bytes 208904 | tf_op jit(solution)/shard_map/ppermute | solution.py:125
  96.5 5.8 %collective-permute-start.20 = (f32[136,128]{1,0:T(8,128)S(1)}, f32[136,128]{1,0:T(8,128)S(1)}, u32[]{:S(2)}, u32[]{:S(2)}) collective-permute-start(f32[136,128]{1,0:T(8,128)S(1)} %shard_map.133.a), channel_id=1, source_target_pairs={{0,16},{8,24},{16,0},{24,8},{1,17},{9,25},{17,1},{25,9},{2,18},{10... | collective-permute-start | bytes 208904 | tf_op jit(solution)/shard_map/ppermute | solution.py:125
  103.1 5.6 %collective-permute-start.24 = (f32[136,128]{1,0:T(8,128)S(1)}, f32[136,128]{1,0:T(8,128)S(1)}, u32[]{:S(2)}, u32[]{:S(2)}) collective-permute-start(f32[136,128]{1,0:T(8,128)S(1)} %shard_map.134.p0), channel_id=1, source_target_pairs={{0,6},{2,4},{4,2},{6,0},{1,7},{3,5},{5,3},{7,1},{8,14},{10,12},{12... | collective-permute-start | bytes 208904 | tf_op jit(solution)/shard_map/ppermute | solution.py:125
  105.8 5.8 %collective-permute-start.23 = (f32[136,128]{1,0:T(8,128)S(1)}, f32[136,128]{1,0:T(8,128)S(1)}, u32[]{:S(2)}, u32[]{:S(2)}) collective-permute-start(f32[136,128]{1,0:T(8,128)S(1)} %shard_map.134.p0), channel_id=1, source_target_pairs={{0,4},{2,6},{4,0},{6,2},{1,5},{3,7},{5,1},{7,3},{8,12},{10,14},{12... | collective-permute-start | bytes 208904 | tf_op jit(solution)/shard_map/ppermute | solution.py:125
  116.4 5.5 %collective-permute-start.27 = (f32[16,640]{1,0:T(8,128)S(1)}, f32[16,640]{1,0:T(8,128)S(1)}, u32[]{:S(2)}, u32[]{:S(2)}) collective-permute-start(f32[16,640]{1,0:T(8,128)S(1)} %pad_maximum_fusion.a0), channel_id=1, source_target_pairs={{0,64},{32,96},{64,0},{96,32},{1,65},{33,97},{65,1},{97,33},{2,66}... | collective-permute-start | bytes 122888 | tf_op jit(solution)/shard_map/ppermute | solution.py:125
  123.5 10.6 %collective-permute-start.29 = (bf16[64,640]{1,0:T(8,128)(2,1)S(1)}, bf16[64,640]{1,0:T(8,128)(2,1)S(1)}, u32[]{:S(2)}, u32[]{:S(2)}) collective-permute-start(bf16[64,640]{1,0:T(8,128)(2,1)S(1)} %get-tuple-element.143), channel_id=1, source_target_pairs={{0,2},{2,0},{4,6},{6,4},{8,10},{10,8},{12,14},{14,12},{16,18},{18,... | collective-permute-start | bytes 245768 | tf_op jit(solution)/shard_map/ppermute | solution.py:478
  123.6 10.5 %collective-permute-start.30 = (bf16[64,640]{1,0:T(8,128)(2,1)S(1)}, bf16[64,640]{1,0:T(8,128)(2,1)S(1)}, u32[]{:S(2)}, u32[]{:S(2)}) collective-permute-start(bf16[64,640]{1,0:T(8,128)(2,1)S(1)} %get-tuple-element.144), channel_id=1, source_target_pairs={{2,4},{6,8},{10,12},{14,16},{18,20},{22,24},{26,28},{30,32},{34,36... | collective-permute-start | bytes 245768 | tf_op jit(solution)/shard_map/ppermute | solution.py:479
  135.8 8.9 %collective-permute-start.31 = (bf16[144,128]{1,0:T(8,128)(2,1)S(1)}, bf16[144,128]{1,0:T(8,128)(2,1)S(1)}, u32[]{:S(2)}, u32[]{:S(2)}) collective-permute-start(bf16[144,128]{1,0:T(8,128)(2,1)S(1)} %get-tuple-element.150), channel_id=1, source_target_pairs={{0,32},{32,0},{64,96},{96,64},{1,33},{33,1},{65,97},{97,65},{2,34}... | collective-permute-start | bytes 110600 | tf_op jit(solution)/shard_map/ppermute | solution.py:125
  141.9 5.5 %collective-permute-start.32 = (bf16[144,128]{1,0:T(8,128)(2,1)S(1)}, bf16[144,128]{1,0:T(8,128)(2,1)S(1)}, u32[]{:S(2)}, u32[]{:S(2)}) collective-permute-start(bf16[144,128]{1,0:T(8,128)(2,1)S(1)} %get-tuple-element.151), channel_id=1, source_target_pairs={{0,64},{32,96},{64,0},{96,32},{1,65},{33,97},{65,1},{97,33},{2,66}... | collective-permute-start | bytes 110600 | tf_op jit(solution)/shard_map/ppermute | solution.py:125
  149.4 5.5 %collective-permute-start.35 = (bf16[144,128]{1,0:T(8,128)(2,1)S(1)}, bf16[144,128]{1,0:T(8,128)(2,1)S(1)}, u32[]{:S(2)}, u32[]{:S(2)}) collective-permute-start(bf16[144,128]{1,0:T(8,128)(2,1)S(1)} %shard_map.140.a), channel_id=1, source_target_pairs={{0,16},{8,24},{16,0},{24,8},{1,17},{9,25},{17,1},{25,9},{2,18},{10... | collective-permute-start | bytes 110600 | tf_op jit(solution)/shard_map/ppermute | solution.py:125
  156.0 5.5 %collective-permute-start.38 = (bf16[144,128]{1,0:T(8,128)(2,1)S(1)}, bf16[144,128]{1,0:T(8,128)(2,1)S(1)}, u32[]{:S(2)}, u32[]{:S(2)}) collective-permute-start(bf16[144,128]{1,0:T(8,128)(2,1)S(1)} %shard_map.141.p0), channel_id=1, source_target_pairs={{0,4},{2,6},{4,0},{6,2},{1,5},{3,7},{5,1},{7,3},{8,12},{10,14},{12... | collective-permute-start | bytes 110600 | tf_op jit(solution)/shard_map/ppermute | solution.py:125
  166.0 5.5 %collective-permute-start.42 = (f32[16,640]{1,0:T(8,128)S(1)}, f32[16,640]{1,0:T(8,128)S(1)}, u32[]{:S(2)}, u32[]{:S(2)}) collective-permute-start(f32[16,640]{1,0:T(8,128)S(1)} %pad_maximum_fusion.1.a0), channel_id=1, source_target_pairs={{0,64},{32,96},{64,0},{96,32},{1,65},{33,97},{65,1},{97,33},{2,66}... | collective-permute-start | bytes 122888 | tf_op jit(solution)/shard_map/ppermute | solution.py:125
  166.0 5.5 %collective-permute-start.41 = (f32[16,640]{1,0:T(8,128)S(1)}, f32[16,640]{1,0:T(8,128)S(1)}, u32[]{:S(2)}, u32[]{:S(2)}) collective-permute-start(f32[16,640]{1,0:T(8,128)S(1)} %pad_maximum_fusion.1.a0), channel_id=1, source_target_pairs={{0,32},{32,0},{64,96},{96,64},{1,33},{33,1},{65,97},{97,65},{2,34}... | collective-permute-start | bytes 122888 | tf_op jit(solution)/shard_map/ppermute | solution.py:125
  173.7 10.1 %collective-permute-start.44 = (bf16[64,640]{1,0:T(8,128)(2,1)S(1)}, bf16[64,640]{1,0:T(8,128)(2,1)S(1)}, u32[]{:S(2)}, u32[]{:S(2)}) collective-permute-start(bf16[64,640]{1,0:T(8,128)(2,1)S(1)} %get-tuple-element.171), channel_id=1, source_target_pairs={{0,2},{2,0},{4,6},{6,4},{8,10},{10,8},{12,14},{14,12},{16,18},{18,... | collective-permute-start | bytes 245768 | tf_op jit(solution)/shard_map/ppermute | solution.py:478
  175.3 8.5 %collective-permute-start.45 = (bf16[64,640]{1,0:T(8,128)(2,1)S(1)}, bf16[64,640]{1,0:T(8,128)(2,1)S(1)}, u32[]{:S(2)}, u32[]{:S(2)}) collective-permute-start(bf16[64,640]{1,0:T(8,128)(2,1)S(1)} %get-tuple-element.172), channel_id=1, source_target_pairs={{2,4},{6,8},{10,12},{14,16},{18,20},{22,24},{26,28},{30,32},{34,36... | collective-permute-start | bytes 245768 | tf_op jit(solution)/shard_map/ppermute | solution.py:479
  184.9 7.4 %collective-permute-start.46 = (bf16[80,128]{1,0:T(8,128)(2,1)S(1)}, bf16[80,128]{1,0:T(8,128)(2,1)S(1)}, u32[]{:S(2)}, u32[]{:S(2)}) collective-permute-start(bf16[80,128]{1,0:T(8,128)(2,1)S(1)} %get-tuple-element.177), channel_id=1, source_target_pairs={{0,32},{32,0},{64,96},{96,64},{1,33},{33,1},{65,97},{97,65},{2,34}... | collective-permute-start | bytes 61448 | tf_op jit(solution)/shard_map/ppermute | solution.py:125
  (43 other events, 340.3 us)
